TPU v7x, 256 devices: a whole 4x4x8 slice. The times are simulated.
256 devices in a mesh: row: 16 (over x, z_lo), col: 16 (over y, z_hi, core).
Axes of the slice: x: 4, y: 4, z: 8 (z_hi: 2, z_lo: 4; z = z_hi * 4 + z_lo), core: 2. Of those that a mesh axis runs over, the one named last changes fastest.
Arguments:
- state: bfloat16 [256, 32768], P(None, ('row', 'col')), may hold values from -0.94921875 to 0.94921875
- adjoint: bfloat16 [256, 32768], P(None, ('col', 'row')), may hold values from -6 to 6
- features: bfloat16 [128, 32768], P(None, ('col', 'row')), may hold values from -6 to 6
- cotangent: bfloat16 [256, 32768], P(None, ('row', 'col')), may hold values from -6 to 6
- mixing: bfloat16 [256, 256], replicated, may hold values from -0.375 to 0.375
- input_weight: bfloat16 [256, 128], replicated, may hold values from -0.5 to 0.5
- tiles: bfloat16 [16, 16, 85, 128, 128], P('row', 'col'), may hold values from -0.0625 to 0.0625
- tile_rows: int32 [16, 16, 85], P('row', 'col'), may hold values from 0 to 15, as said below
- tile_cols: int32 [16, 16, 85], P('row', 'col'), may hold values from 0 to 15, as said below
- live_tiles: int32 [16, 16], P('row', 'col'), may hold values from 42 to 85, as said below
Outputs:
- new_state: bfloat16 [256, 32768], P(None, ('col', 'row'))
- new_adjoint: bfloat16 [256, 32768], P(None, ('row', 'col'))
Inputs may be any that keep to these rules, and one draw needn't show every extreme that they name: On one device the pairs (tile_rows, tile_cols) of its 85 slots are all different. `tile_cols`: see tile_rows. `live_tiles`: some device has all 85 slots live.
All inputs are finite; a program needn't handle non-finite values.
Results may differ from a plain program's by a relative error of at most 0.014.
Values may be sent and summed in bfloat16 or wider, within the bound.
A program may use at most 64 MiB of HBM per device.

v0:
```python
import jax
import jax.numpy as jnp
from jax import lax
from jax.sharding import PartitionSpec as P


def split_up(shard, dim, size):
    before, after = (shard.shape[:dim], shard.shape[dim + 1 :])
    return jnp.moveaxis(shard.reshape(*before, size, -1, *after), dim, 0)


def summed_on_arrival(shard, axis, dim):
    size = lax.axis_size(axis)
    blocks = lax.all_to_all(split_up(shard, dim, size), axis, 0, 0, tiled=True)
    return jnp.sum(blocks.astype(jnp.float32), axis=0)


def copy_for_each(shard, axis):
    copies = jnp.broadcast_to(shard, (lax.axis_size(axis), *shard.shape))
    return lax.all_to_all(copies, axis, split_axis=0, concat_axis=0, tiled=True)


def laid_out(blocks, dim):
    shape = list(blocks.shape[1:])
    shape[dim] *= blocks.shape[0]
    return jnp.moveaxis(blocks, 0, dim).reshape(shape)


def gathered_copies(shard, axis, dim):
    blocks = copy_for_each(shard, axis)
    return laid_out(blocks, dim)


def sweep_slots(limit, slots, group, turn_fn, initial):

    def turn(number, total):
        first = number * group
        start = jnp.minimum(first, slots - group)
        return turn_fn(total, start, first)

    return lax.fori_loop(0, limit, turn, initial)


def slot_window(slab, rows, cols, count, start, first, group):
    slot_tiles = lax.dynamic_slice_in_dim(slab, start, group, 0)
    slot_rows = lax.dynamic_slice_in_dim(rows, start, group, 0)
    slot_cols = lax.dynamic_slice_in_dim(cols, start, group, 0)
    slot_ids = start + jnp.arange(group, dtype=jnp.int32)
    live = ((slot_ids >= first) & (slot_ids < count)).astype(jnp.float32)
    return (slot_tiles, slot_rows, slot_cols, live)


def per_device(
    state,
    adjoint,
    features,
    cotangent,
    mixing,
    input_weight,
    tiles,
    tile_rows,
    tile_cols,
    live_tiles,
):
    slab = tiles[0, 0]
    rows = tile_rows[0, 0]
    cols = tile_cols[0, 0]
    count = live_tiles[0, 0]
    hidden, nodes = state.shape
    side = slab.shape[-1]
    slots = slab.shape[0]
    group = min(32, slots)
    row_blocks = nodes * lax.axis_size("col") // side
    col_blocks = nodes * lax.axis_size("row") // side
    limit = (slots + group - 1) // group

    def forward_part(whole, total, slot_tiles, slot_rows, slot_cols, live):
        picked = jnp.take(whole, slot_rows, axis=1)
        terms = jnp.einsum("hsk,skn->hsn", picked, slot_tiles, preferred_element_type=jnp.float32)
        return total.at[:, slot_cols].add(terms * live[None, :, None])

    def backward_part(whole, total, slot_tiles, slot_rows, slot_cols, live):
        picked = jnp.take(whole, slot_cols, axis=1)
        terms = jnp.einsum("hsn,skn->hsk", picked, slot_tiles, preferred_element_type=jnp.float32)
        return total.at[:, slot_rows].add(terms * live[None, :, None])

    def round_partial(partial_value):
        narrow = lax.optimization_barrier(partial_value.astype(jnp.bfloat16))
        return narrow.astype(jnp.float32)

    forward_zero = jnp.zeros((hidden, col_blocks, side), jnp.float32)
    backward_zero = jnp.zeros((hidden, row_blocks, side), jnp.float32)
    whole_state = gathered_copies(state, "col", 1).reshape(hidden, row_blocks, side)
    whole_adjoint = gathered_copies(adjoint, "row", 1).reshape(hidden, col_blocks, side)

    def forward_turn(total, start, first):
        window = slot_window(slab, rows, cols, count, start, first, group)
        return forward_part(whole_state, total, *window)

    forward_total = sweep_slots(limit, slots, group, forward_turn, forward_zero)
    partial_value = forward_total.reshape(hidden, col_blocks * side)
    partial_value = round_partial(partial_value)
    summed = summed_on_arrival(partial_value.astype(jnp.bfloat16), "row", 1)
    flow = summed.astype(jnp.bfloat16)
    pre = jnp.dot(mixing, flow, preferred_element_type=jnp.float32)
    pre = pre + jnp.dot(input_weight, features, preferred_element_type=jnp.float32)
    new_state = jnp.tanh(pre).astype(jnp.bfloat16)

    def backward_turn(total, start, first):
        window = slot_window(slab, rows, cols, count, start, first, group)
        return backward_part(whole_adjoint, total, *window)

    backward_total = sweep_slots(limit, slots, group, backward_turn, backward_zero)
    partial_value = backward_total.reshape(hidden, row_blocks * side)
    partial_value = round_partial(partial_value)
    summed = summed_on_arrival(partial_value.astype(jnp.bfloat16), "col", 1)
    back = summed.astype(jnp.bfloat16)
    state_wide = state.astype(jnp.float32)
    slope = 1.0 - state_wide * state_wide
    pulled = jnp.dot(mixing.T, back, preferred_element_type=jnp.float32)
    new_adjoint = (slope * (pulled + cotangent.astype(jnp.float32))).astype(jnp.bfloat16)
    return (new_state, new_adjoint)


def solution(mesh):
    placed = (
        P(None, ("row", "col")),
        P(None, ("col", "row")),
        P(None, ("col", "row")),
        P(None, ("row", "col")),
        P(),
        P(),
        P("row", "col", None, None, None),
        P("row", "col", None),
        P("row", "col", None),
        P("row", "col"),
    )
    return jax.shard_map(
        per_device,
        mesh=mesh,
        in_specs=placed,
        out_specs=(P(None, ("col", "row")), P(None, ("row", "col"))),
        check_vma=False,
    )
```

profile of v0, /device:TPU:32, one launch (start us, length us, event | category | flops | bytes accessed | tf_op | source)
XLA Modules:
  0.0 221.7 jit_solution(5541448885835930740)
XLA Ops:
  2.7 10.3 %all-to-all-start = ((bf16[16,256,128]{2,1,0:T(8,128)(2,1)}), bf16[16,256,128]{2,1,0:T(8,128)(2,1)S(1)}, u32[]{:S(2)}, u32[]{:S(2)}) async-start(bf16[16,256,128]{2,1,0:T(8,128)(2,1)} %broadcast_in_dim.35), calls=%async_computation | async-start | bytes 2097152 | tf_op jit(solution)/shard_map/all_to_all | solution.py:20
  13.0 31.6 %all-to-all-done = bf16[16,256,128]{2,1,0:T(8,128)(2,1)S(1)} async-done(((bf16[16,256,128]{2,1,0:T(8,128)(2,1)}), bf16[16,256,128]{2,1,0:T(8,128)(2,1)S(1)}, u32[]{:S(2)}, u32[]{:S(2)}) %all-to-all-start) | async-done | bytes 1048608 | tf_op jit(solution)/shard_map/all_to_all | solution.py:20
  46.0 6.4 %all-to-all-start.2 = ((bf16[16,256,128]{2,1,0:T(8,128)(2,1)}), bf16[16,256,128]{2,1,0:T(8,128)(2,1)S(1)}, u32[]{:S(2)}, u32[]{:S(2)}) async-start(bf16[16,256,128]{2,1,0:T(8,128)(2,1)} %broadcast_in_dim.36), calls=%async_computation.2 | async-start | bytes 2097152 | tf_op jit(solution)/shard_map/all_to_all | solution.py:20
  52.6 63.2 %while.26 = (s32[]{:T(128)}, f32[256,16,128]{2,0,1:T(8,128)S(1)}, s32[85]{0:T(128)S(1)}, bf16[85,128,128]{2,1,0:T(8,128)(2,1)}, s32[85]{0:T(128)S(1)}, /*index=5...) while((s32[]{:T(128)}, f32[256,16,128]{2,0,1:T(8,128)S(1)}, ...), condition=%wide.region_2.0_spmd, body=%wide.region_0.3_spmd.sunk | while | flops 271582656 | bytes 32511368 | solution.py:41
  56.7 4.8 %multiply_bitcast_fusion.4 = f32[32,256,128]{1,2,0:T(8,128)} fusion(bf16[32,256,128]{2,1,0:T(8,128)(2,1)} %gather_fusion, f32[32]{0:T(128)S(1)} %get-tuple-element.400, pred[32]{0:T(512)(128)(4,1)S(1)} %get-tuple-element.401, bf16[85,128,128]{2,1,0:T(8,128)(2,1)} %get-tuple-element.439, s32[]{:T(128)S(6)} %select_n.69), kind=kOutput, calls=%fused_computation.4.clone.1 | convolution fusion | flops 270532608 | bytes 7340196 | tf_op jit(solution)/shard_map/while/body/eval_jaxpr/hsk,skn->hsn/dot_general | solution.py:79
  61.5 5.6 %copy.46 = f32[32,256,128]{2,1,0:T(8,128)} copy(f32[32,256,128]{1,2,0:T(8,128)} %multiply_bitcast_fusion.4) | data formatting | bytes 8388608 | tf_op jit(solution)/shard_map/while/body/eval_jaxpr/mul | solution.py:80
  67.2 6.5 %scatter_fusion = f32[256,16,128]{2,0,1:T(8,128)S(1)} fusion(f32[256,16,128]{2,0,1:T(8,128)S(1)} %get-tuple-element.425, s32[32]{0:T(128)S(1)} %compare_select_fusion.8, f32[32,256,128]{2,1,0:T(8,128)} %copy.46), kind=kCustom, calls=%fused_computation.2.clone.1 | custom fusion | flops 1048576 | bytes 12583040 | tf_op jit(solution)/shard_map/while/body/eval_jaxpr/scatter-add | solution.py:80
  77.8 4.8 %multiply_bitcast_fusion.4 = f32[32,256,128]{1,2,0:T(8,128)} fusion(bf16[32,256,128]{2,1,0:T(8,128)(2,1)} %gather_fusion, f32[32]{0:T(128)S(1)} %get-tuple-element.400, pred[32]{0:T(512)(128)(4,1)S(1)} %get-tuple-element.401, bf16[85,128,128]{2,1,0:T(8,128)(2,1)} %get-tuple-element.439, s32[]{:T(128)S(6)} %select_n.69), kind=kOutput, calls=%fused_computation.4.clone.1 | convolution fusion | flops 270532608 | bytes 7340196 | tf_op jit(solution)/shard_map/while/body/eval_jaxpr/hsk,skn->hsn/dot_general | solution.py:79
  82.5 5.6 %copy.46 = f32[32,256,128]{2,1,0:T(8,128)} copy(f32[32,256,128]{1,2,0:T(8,128)} %multiply_bitcast_fusion.4) | data formatting | bytes 8388608 | tf_op jit(solution)/shard_map/while/body/eval_jaxpr/mul | solution.py:80
  88.2 6.5 %scatter_fusion = f32[256,16,128]{2,0,1:T(8,128)S(1)} fusion(f32[256,16,128]{2,0,1:T(8,128)S(1)} %get-tuple-element.425, s32[32]{0:T(128)S(1)} %compare_select_fusion.8, f32[32,256,128]{2,1,0:T(8,128)} %copy.46), kind=kCustom, calls=%fused_computation.2.clone.1 | custom fusion | flops 1048576 | bytes 12583040 | tf_op jit(solution)/shard_map/while/body/eval_jaxpr/scatter-add | solution.py:80
  98.8 4.8 %multiply_bitcast_fusion.4 = f32[32,256,128]{1,2,0:T(8,128)} fusion(bf16[32,256,128]{2,1,0:T(8,128)(2,1)} %gather_fusion, f32[32]{0:T(128)S(1)} %get-tuple-element.400, pred[32]{0:T(512)(128)(4,1)S(1)} %get-tuple-element.401, bf16[85,128,128]{2,1,0:T(8,128)(2,1)} %get-tuple-element.439, s32[]{:T(128)S(6)} %select_n.69), kind=kOutput, calls=%fused_computation.4.clone.1 | convolution fusion | flops 270532608 | bytes 7340196 | tf_op jit(solution)/shard_map/while/body/eval_jaxpr/hsk,skn->hsn/dot_general | solution.py:79
  103.6 5.6 %copy.46 = f32[32,256,128]{2,1,0:T(8,128)} copy(f32[32,256,128]{1,2,0:T(8,128)} %multiply_bitcast_fusion.4) | data formatting | bytes 8388608 | tf_op jit(solution)/shard_map/while/body/eval_jaxpr/mul | solution.py:80
  109.3 6.5 %scatter_fusion = f32[256,16,128]{2,0,1:T(8,128)S(1)} fusion(f32[256,16,128]{2,0,1:T(8,128)S(1)} %get-tuple-element.425, s32[32]{0:T(128)S(1)} %compare_select_fusion.8, f32[32,256,128]{2,1,0:T(8,128)} %copy.46), kind=kCustom, calls=%fused_computation.2.clone.1 | custom fusion | flops 1048576 | bytes 12583040 | tf_op jit(solution)/shard_map/while/body/eval_jaxpr/scatter-add | solution.py:80
  117.1 7.5 %all-to-all-start.1 = ((bf16[16,256,128]{1,2,0:T(8,128)(2,1)}), bf16[16,256,128]{1,2,0:T(8,128)(2,1)}, u32[]{:S(2)}, u32[]{:S(2)}) async-start(bf16[16,256,128]{1,2,0:T(8,128)(2,1)} %bitcast.57), calls=%async_computation.1 | async-start | bytes 2097152 | tf_op jit(solution)/shard_map/all_to_all | solution.py:14
  124.8 59.1 %while.27 = (s32[]{:T(128)}, f32[256,16,128]{2,0,1:T(8,128)S(1)}, s32[85]{0:T(128)S(1)}, bf16[85,128,128]{2,1,0:T(8,128)(2,1)}, s32[85]{0:T(128)S(1)}, /*index=5...) while((s32[]{:T(128)}, f32[256,16,128]{2,0,1:T(8,128)S(1)}, ...), condition=%wide.region_6.0_spmd, body=%wide.region_4.0_spmd.sunk | while | flops 271582656 | bytes 32511368 | solution.py:41
  127.7 4.7 %multiply_bitcast_fusion.5 = f32[32,256,128]{1,2,0:T(8,128)} fusion(bf16[32,256,128]{2,1,0:T(8,128)(2,1)} %gather_fusion.1, f32[32]{0:T(128)S(1)} %get-tuple-element.410, pred[32]{0:T(512)(128)(4,1)S(1)} %get-tuple-element.411, bf16[85,128,128]{2,1,0:T(8,128)(2,1)} %get-tuple-element.475, s32[]{:T(128)S(6)} %select_n.72), kind=kOutput, calls=%fused_computation.17.clone.1 | convolution fusion | flops 270532608 | bytes 7340196 | tf_op jit(solution)/shard_map/while/body/eval_jaxpr/hsn,skn->hsk/dot_general | solution.py:84
  132.4 5.6 %copy.47 = f32[32,256,128]{2,1,0:T(8,128)} copy(f32[32,256,128]{1,2,0:T(8,128)} %multiply_bitcast_fusion.5) | data formatting | bytes 8388608 | tf_op jit(solution)/shard_map/while/body/eval_jaxpr/mul | solution.py:85
  138.1 6.5 %scatter_fusion.1 = f32[256,16,128]{2,0,1:T(8,128)S(1)} fusion(f32[256,16,128]{2,0,1:T(8,128)S(1)} %get-tuple-element.461, s32[32]{0:T(128)S(1)} %compare_select_fusion.9, f32[32,256,128]{2,1,0:T(8,128)} %copy.47), kind=kCustom, calls=%fused_computation.3.clone.1 | custom fusion | flops 1048576 | bytes 12583040 | tf_op jit(solution)/shard_map/while/body/eval_jaxpr/scatter-add | solution.py:85
  147.5 4.7 %multiply_bitcast_fusion.5 = f32[32,256,128]{1,2,0:T(8,128)} fusion(bf16[32,256,128]{2,1,0:T(8,128)(2,1)} %gather_fusion.1, f32[32]{0:T(128)S(1)} %get-tuple-element.410, pred[32]{0:T(512)(128)(4,1)S(1)} %get-tuple-element.411, bf16[85,128,128]{2,1,0:T(8,128)(2,1)} %get-tuple-element.475, s32[]{:T(128)S(6)} %select_n.72), kind=kOutput, calls=%fused_computation.17.clone.1 | convolution fusion | flops 270532608 | bytes 7340196 | tf_op jit(solution)/shard_map/while/body/eval_jaxpr/hsn,skn->hsk/dot_general | solution.py:84
  152.1 5.6 %copy.47 = f32[32,256,128]{2,1,0:T(8,128)} copy(f32[32,256,128]{1,2,0:T(8,128)} %multiply_bitcast_fusion.5) | data formatting | bytes 8388608 | tf_op jit(solution)/shard_map/while/body/eval_jaxpr/mul | solution.py:85
  157.8 6.5 %scatter_fusion.1 = f32[256,16,128]{2,0,1:T(8,128)S(1)} fusion(f32[256,16,128]{2,0,1:T(8,128)S(1)} %get-tuple-element.461, s32[32]{0:T(128)S(1)} %compare_select_fusion.9, f32[32,256,128]{2,1,0:T(8,128)} %copy.47), kind=kCustom, calls=%fused_computation.3.clone.1 | custom fusion | flops 1048576 | bytes 12583040 | tf_op jit(solution)/shard_map/while/body/eval_jaxpr/scatter-add | solution.py:85
  171.8 5.6 %copy.47 = f32[32,256,128]{2,1,0:T(8,128)} copy(f32[32,256,128]{1,2,0:T(8,128)} %multiply_bitcast_fusion.5) | data formatting | bytes 8388608 | tf_op jit(solution)/shard_map/while/body/eval_jaxpr/mul | solution.py:85
  177.5 6.5 %scatter_fusion.1 = f32[256,16,128]{2,0,1:T(8,128)S(1)} fusion(f32[256,16,128]{2,0,1:T(8,128)S(1)} %get-tuple-element.461, s32[32]{0:T(128)S(1)} %compare_select_fusion.9, f32[32,256,128]{2,1,0:T(8,128)} %copy.47), kind=kCustom, calls=%fused_computation.3.clone.1 | custom fusion | flops 1048576 | bytes 12583040 | tf_op jit(solution)/shard_map/while/body/eval_jaxpr/scatter-add | solution.py:85
  191.9 28.8 %all-to-all-done.3 = bf16[16,256,128]{1,2,0:T(8,128)(2,1)S(1)} async-done(((bf16[16,256,128]{1,2,0:T(8,128)(2,1)}), bf16[16,256,128]{1,2,0:T(8,128)(2,1)S(1)}, u32[]{:S(2)}, u32[]{:S(2)}) %all-to-all-start.3) | async-done | bytes 1048608 | tf_op jit(solution)/shard_map/all_to_all | solution.py:14
  (61 shorter events, 40.0 us)
Async XLA Ops:
  0.6 190.3 %copy-start = (bf16[256,256]{1,0:T(8,128)(2,1)S(1)}, bf16[256,256]{1,0:T(8,128)(2,1)}, u32[]{:S(2)}) copy-start(bf16[256,256]{1,0:T(8,128)(2,1)} %param.20) | copy-start | bytes 393220
  0.6 44.0 %copy-start.3 = (bf16[256,128]{1,0:T(8,128)(2,1)S(1)}, bf16[256,128]{1,0:T(8,128)(2,1)}, u32[]{:S(2)}) copy-start(bf16[256,128]{1,0:T(8,128)(2,1)} %param.17) | copy-start | bytes 196612
  2.7 41.9 %all-to-all-start = ((bf16[16,256,128]{2,1,0:T(8,128)(2,1)}), bf16[16,256,128]{2,1,0:T(8,128)(2,1)S(1)}, u32[]{:S(2)}, u32[]{:S(2)}) async-start(bf16[16,256,128]{2,1,0:T(8,128)(2,1)} %broadcast_in_dim.35), calls=%async_computation | async-start | bytes 2097152 | tf_op jit(solution)/shard_map/all_to_all | solution.py:20
  44.6 7.7 %copy-start.1 = (bf16[16,256,128]{2,1,0:T(8,128)(2,1)}, bf16[16,256,128]{2,1,0:T(8,128)(2,1)S(1)}, u32[]{:S(2)}) copy-start(bf16[16,256,128]{2,1,0:T(8,128)(2,1)S(1)} %all-to-all-done) | copy-start | bytes 3145732
  46.0 6.6 %copy-start.7 = (s32[1,1,85]{2,1,0:T(1,128)S(1)}, s32[1,1,85]{2,1,0:T(1,128)}, u32[]{:S(2)}) copy-start(s32[1,1,85]{2,1,0:T(1,128)} %param.24) | copy-start | bytes 1024
  46.0 6.6 %copy-start.8 = (s32[1,1,85]{2,1,0:T(1,128)S(1)}, s32[1,1,85]{2,1,0:T(1,128)}, u32[]{:S(2)}) copy-start(s32[1,1,85]{2,1,0:T(1,128)} %param.23) | copy-start | bytes 1024
  46.0 71.1 %all-to-all-start.2 = ((bf16[16,256,128]{2,1,0:T(8,128)(2,1)}), bf16[16,256,128]{2,1,0:T(8,128)(2,1)S(1)}, u32[]{:S(2)}, u32[]{:S(2)}) async-start(bf16[16,256,128]{2,1,0:T(8,128)(2,1)} %broadcast_in_dim.36), calls=%async_computation.2 | async-start | bytes 2097152 | tf_op jit(solution)/shard_map/all_to_all | solution.py:20
  117.1 68.3 %all-to-all-start.1 = ((bf16[16,256,128]{1,2,0:T(8,128)(2,1)}), bf16[16,256,128]{1,2,0:T(8,128)(2,1)}, u32[]{:S(2)}, u32[]{:S(2)}) async-start(bf16[16,256,128]{1,2,0:T(8,128)(2,1)} %bitcast.57), calls=%async_computation.1 | async-start | bytes 2097152 | tf_op jit(solution)/shard_map/all_to_all | solution.py:14
  184.0 5.1 %copy-start.2 = (bf16[256,128]{1,0:T(8,128)(2,1)S(1)}, bf16[256,128]{1,0:T(8,128)(2,1)}, u32[]{:S(2)}) copy-start(bf16[256,128]{1,0:T(8,128)(2,1)} %param.16) | copy-start | bytes 196612
  184.0 5.2 %copy-start.5 = (bf16[256,128]{1,0:T(8,128)(2,1)S(1)}, bf16[256,128]{1,0:T(8,128)(2,1)}, u32[]{:S(2)}) copy-start(bf16[256,128]{1,0:T(8,128)(2,1)} %param.19) | copy-start | bytes 196612
  184.0 5.3 %copy-start.4 = (bf16[256,128]{1,0:T(8,128)(2,1)S(1)}, bf16[256,128]{1,0:T(8,128)(2,1)}, u32[]{:S(2)}) copy-start(bf16[256,128]{1,0:T(8,128)(2,1)} %param.21) | copy-start | bytes 196612
  184.0 5.3 %copy-start.6 = (bf16[128,128]{1,0:T(8,128)(2,1)S(1)}, bf16[128,128]{1,0:T(8,128)(2,1)}, u32[]{:S(2)}) copy-start(bf16[128,128]{1,0:T(8,128)(2,1)} %param.18) | copy-start | bytes 98308
  185.4 35.2 %all-to-all-start.3 = ((bf16[16,256,128]{1,2,0:T(8,128)(2,1)}), bf16[16,256,128]{1,2,0:T(8,128)(2,1)S(1)}, u32[]{:S(2)}, u32[]{:S(2)}) async-start(bf16[16,256,128]{1,2,0:T(8,128)(2,1)} %bitcast.16), calls=%async_computation.3 | async-start | bytes 2097152 | tf_op jit(solution)/shard_map/all_to_all | solution.py:14
where the time goes:
time: 223 us; the launch traced here: 222 us
  waiting for transfers between devices  60.4 us (27%)
  local copies, waits for them, and re-layouts  58.4 us (26%)
  other arithmetic  45.3 us (20%)
  matrix products  28.9 us (13%)
  starting transfers between devices  27.8 us (12%)
    all_to_all x2, waiting for transfers between devices, copy_for_each(): return lax.all_to_all(copies, axis, split_axis=0, concat_axis=0, tiled=True)  31.6 us
    all_to_all x2, waiting for transfers between devices, summed_on_arrival(): blocks = lax.all_to_all(split_up(shard, dim, size), axis, 0, 0, tiled=True)  28.8 us
    scatter-add x3, other arithmetic, forward_part(): return total.at[:, slot_cols].add(terms * live[None, :, None])  19.4 us
    scatter-add x3, other arithmetic, backward_part(): return total.at[:, slot_rows].add(terms * live[None, :, None])  19.4 us
    mul x3, local copies, waits for them, and re-layouts, forward_part(): return total.at[:, slot_cols].add(terms * live[None, :, None])  16.8 us
    mul x3, local copies, waits for them, and re-layouts, backward_part(): return total.at[:, slot_rows].add(terms * live[None, :, None])  16.8 us
    all_to_all x2, starting transfers between devices, copy_for_each(): return lax.all_to_all(copies, axis, split_axis=0, concat_axis=0, tiled=True)  16.7 us
    dot_general x3, matrix products, forward_part(): jnp.einsum('hsk,skn->hsn', picked, slot_tiles, preferred_element_type=jnp...  14.3 us
  transfers between devices with their start and end apart: 4, of which 2 were waited for; matrix products, arithmetic and copies ran while one was open for 58% of the time, Pallas kernels for 0%

commit v1 on v0

v1 whole, which is shorter than its diff:
```python
import functools

import jax
import jax.numpy as jnp
from jax import lax
from jax.experimental import pallas as pl
from jax.experimental.pallas import tpu as pltpu
from jax.sharding import PartitionSpec as P

SIDE = 128
BF16 = jnp.bfloat16
F32 = jnp.float32
COPIES = 72


def slot_table(rows, cols, count, blocks):
    slots = rows.shape[0]
    ids = jnp.arange(slots, dtype=jnp.int32)
    places = rows * blocks + cols
    here = (places[None, :] == jnp.arange(blocks * blocks, dtype=jnp.int32)[:, None]) & (ids < count)[None, :]
    return slots + jnp.sum(jnp.where(here, ids[None, :] - slots, 0), axis=1, dtype=jnp.int32)


def kernel(
    slot_of,
    state_hbm,
    adjoint_hbm,
    features,
    cotangent,
    mixing,
    input_weight,
    tiles_hbm,
    new_state,
    new_adjoint,
    tiles,
    dense,
    states,
    adjoints,
    fpart,
    bpart,
    fhalf_up,
    fhalf_down,
    ffull_up,
    ffull_down,
    fsum,
    fin,
    bcore,
    bhalf_up,
    bhalf_down,
    bfull_up,
    bfull_down,
    bsum,
    bin_,
    local_sems,
    send_sems,
    recv_sems,
):
    row = lax.axis_index("row")
    col = lax.axis_index("col")
    x, zl = row // 4, row % 4
    y, zh, core = col // 4, (col // 2) % 2, col % 2
    slots = tiles_hbm.shape[0]

    def row_of(dx, dz):
        return ((x + dx) % 4) * 4 + (zl + dz) % 4

    def col_of(dy, dh, dk):
        return ((y + dy) % 4) * 4 + ((zh + dh) % 2) * 2 + (core + dk) % 2

    def to_row(dx, dz):
        return {"row": row_of(dx, dz), "col": col}

    def to_col(dy, dh, dk):
        return {"row": row, "col": col_of(dy, dh, dk)}

    partners = [to_col(0, 0, 1), to_col(0, 1, 0), to_col(1, 0, 0), to_col(3, 0, 0)]
    partners += [to_row(1, 0), to_row(3, 0), to_row(0, 1), to_row(0, 2), to_row(0, 3)]
    barrier = pltpu.get_barrier_semaphore()
    for partner in partners:
        pl.semaphore_signal(barrier, inc=1, device_id=partner, device_id_type=pl.DeviceIdType.MESH)

    sent = []
    names = {}

    def number(name):
        return names.setdefault(name, len(names))

    def send(name, src, dst, device):
        n = number(name)
        copy = pltpu.make_async_remote_copy(
            src_ref=src,
            dst_ref=dst,
            send_sem=send_sems.at[n],
            recv_sem=recv_sems.at[n],
            device_id=device,
            device_id_type=pl.DeviceIdType.MESH,
        )
        copy.start()
        sent.append(copy)

    def arrived(name, ref):
        n = number(name)
        pltpu.make_async_remote_copy(
            src_ref=ref,
            dst_ref=ref,
            send_sem=send_sems.at[n],
            recv_sem=recv_sems.at[n],
            device_id=partners[0],
            device_id_type=pl.DeviceIdType.MESH,
        ).wait_recv()

    upper, lower = pl.ds(0, 128), pl.ds(128, 128)

    tile_copy = pltpu.make_async_copy(tiles_hbm, tiles.at[pl.ds(0, slots)], local_sems.at[0])
    state_copy = pltpu.make_async_copy(state_hbm, states.at[col], local_sems.at[1])
    adjoint_copy = pltpu.make_async_copy(adjoint_hbm, adjoints.at[row], local_sems.at[2])
    state_copy.start()
    adjoint_copy.start()
    tile_copy.start()
    tiles[slots] = jnp.zeros((SIDE, SIDE), BF16)
    pl.semaphore_wait(barrier, len(partners))

    send("s_z", state_hbm, states.at[col], to_col(0, 1, 0))
    for d in (1, 3, 2):
        send(f"a_z{d}", adjoint_hbm, adjoints.at[row], to_row(0, d))
    send("s_up0", state_hbm, states.at[col], to_col(1, 0, 0))
    send("s_dn0", state_hbm, states.at[col], to_col(3, 0, 0))
    send("a_up0", adjoint_hbm, adjoints.at[row], to_row(1, 0))
    send("a_dn0", adjoint_hbm, adjoints.at[row], to_row(3, 0))
    send("s_k00", state_hbm, states.at[col], to_col(0, 0, 1))

    tile_copy.wait()
    blocks = dense.shape[0] // SIDE

    def place(r, carry):
        start = pl.multiple_of(r * SIDE, SIDE)
        for c in range(blocks):
            dense[pl.ds(start, SIDE), c * SIDE : (c + 1) * SIDE] = tiles[slot_of[r * blocks + c]]
        return carry

    lax.fori_loop(0, blocks, place, 0)

    block = states.at[col_of(0, 1, 0)]
    arrived("s_z", block)
    send("s_up1", block, block, to_col(1, 0, 0))
    send("s_dn1", block, block, to_col(3, 0, 0))
    send("s_k01", block, block, to_col(0, 0, 1))
    for d in (1, 3, 2):
        block = adjoints.at[row_of(0, 4 - d)]
        arrived(f"a_z{d}", block)
        send(f"a_up{d}", block, block, to_row(1, 0))
        send(f"a_dn{d}", block, block, to_row(3, 0))

    for h in (0, 1):
        block = states.at[col_of(3, h, 0)]
        arrived(f"s_up{h}", block)
        send(f"s_far_up{h}", block.at[upper], block.at[upper], to_col(1, 0, 0))
        send(f"s_k1{h}", block, block, to_col(0, 0, 1))
        block = states.at[col_of(1, h, 0)]
        arrived(f"s_dn{h}", block)
        send(f"s_far_dn{h}", block.at[lower], block.at[lower], to_col(3, 0, 0))
        send(f"s_k3{h}", block, block, to_col(0, 0, 1))
    for d in (0, 1, 3, 2):
        block = adjoints.at[row_of(3, 4 - d)]
        arrived(f"a_up{d}", block)
        send(f"a_far_up{d}", block.at[upper], block.at[upper], to_row(1, 0))
        block = adjoints.at[row_of(1, 4 - d)]
        arrived(f"a_dn{d}", block)
        send(f"a_far_dn{d}", block.at[lower], block.at[lower], to_row(3, 0))
    for h in (0, 1):
        block = states.at[col_of(2, h, 0)]
        arrived(f"s_far_up{h}", block.at[upper])
        arrived(f"s_far_dn{h}", block.at[lower])
        send(f"s_k2{h}", block, block, to_col(0, 0, 1))
    for h in (0, 1):
        for dy in range(4):
            arrived(f"s_k{dy}{h}", states.at[col_of((4 - dy) % 4 if dy in (1, 3) else dy, h, 1)])
    state_copy.wait()

    def forward(first):
        whole = jnp.concatenate([states[i] for i in range(blocks)], axis=1)
        start = pl.multiple_of(first * SIDE, SIDE)
        product = jnp.dot(whole, dense[:, pl.ds(start, 4 * SIDE)], preferred_element_type=F32)
        for i in range(4):
            fpart[first + i] = product[:, i * SIDE : (i + 1) * SIDE].astype(BF16)

    def fset(dx):
        return fpart.at[pl.ds(((x + dx) % 4) * 4, 4)]

    def forward_turn(i, carry):
        forward(((x + 2 + i) % 4) * 4)
        return carry

    forward(((x + 2) % 4) * 4)
    send("f_half_up", fset(2).at[:, upper], fhalf_up, to_row(1, 0))
    send("f_half_dn", fset(2).at[:, lower], fhalf_down, to_row(3, 0))
    forward(((x + 1) % 4) * 4)
    forward(((x + 3) % 4) * 4)
    arrived("f_half_up", fhalf_up)
    mine = fset(1)
    mine[:, 0:128] = (mine[:, 0:128].astype(F32) + fhalf_up[...].astype(F32)).astype(BF16)
    send("f_full_up", mine, ffull_up, to_row(1, 0))
    arrived("f_half_dn", fhalf_down)
    mine = fset(3)
    mine[:, 128:256] = (mine[:, 128:256].astype(F32) + fhalf_down[...].astype(F32)).astype(BF16)
    send("f_full_dn", mine, ffull_down, to_row(3, 0))
    forward(x * 4)

    for d in (0, 1, 3, 2):
        block = adjoints.at[row_of(2, 4 - d)]
        arrived(f"a_far_up{d}", block.at[upper])
        arrived(f"a_far_dn{d}", block.at[lower])
    adjoint_copy.wait()

    def backward(first):
        whole = jnp.concatenate([adjoints[i] for i in range(blocks)], axis=1)
        start = pl.multiple_of(first * SIDE, SIDE)
        product = lax.dot_general(
            whole, dense[pl.ds(start, 4 * SIDE), :], (((1,), (1,)), ((), ())), preferred_element_type=F32
        )
        for i in range(4):
            bpart[i % 2, first // 2 + i // 2] = product[:, i * SIDE : (i + 1) * SIDE].astype(BF16)

    for dy in (2, 1, 3, 0):
        where = ((y + dy) % 4) * 2
        backward(where * 2)
        send(f"b_k{dy}", bpart.at[1 - core, pl.ds(where, 2)], bcore.at[pl.ds(where, 2)], to_col(0, 0, 1))

    arrived("f_full_up", ffull_up)
    arrived("f_full_dn", ffull_down)
    for d in (1, 3, 2, 0):
        place_ = (zl + d) % 4
        total = fpart[x * 4 + place_].astype(F32) + ffull_up[place_].astype(F32) + ffull_down[place_].astype(F32)
        if d:
            fsum[d - 1] = total.astype(BF16)
            send(f"f_z{d}", fsum.at[d - 1], fin.at[d - 1], to_row(0, d))
        else:
            fsum[3] = total.astype(BF16)

    def over_cores(dy):
        where = ((y + dy) % 4) * 2
        arrived(f"b_k{dy}", bcore.at[pl.ds(where, 2)])
        for i in range(2):
            bcore[where + i] = (bcore[where + i].astype(F32) + bpart[core, where + i].astype(F32)).astype(BF16)
        return bcore.at[pl.ds(where, 2)]

    far = over_cores(2)
    send("b_half_up", far.at[:, upper], bhalf_up, to_col(1, 0, 0))
    send("b_half_dn", far.at[:, lower], bhalf_down, to_col(3, 0, 0))
    near = over_cores(1)
    arrived("b_half_up", bhalf_up)
    near[:, 0:128] = (near[:, 0:128].astype(F32) + bhalf_up[...].astype(F32)).astype(BF16)
    send("b_full_up", near, bfull_up, to_col(1, 0, 0))
    near = over_cores(3)
    arrived("b_half_dn", bhalf_down)
    near[:, 128:256] = (near[:, 128:256].astype(F32) + bhalf_down[...].astype(F32)).astype(BF16)
    send("b_full_dn", near, bfull_down, to_col(3, 0, 0))
    over_cores(0)
    arrived("b_full_up", bfull_up)
    arrived("b_full_dn", bfull_down)
    for h in (1, 0):
        place_ = (zh + h) % 2
        total = bcore[y * 2 + place_].astype(F32) + bfull_up[place_].astype(F32) + bfull_down[place_].astype(F32)
        bsum[h] = total.astype(BF16)
        if h:
            send("b_z", bsum.at[1], bin_, to_col(0, 1, 0))

    total = fsum[3].astype(F32)
    for d in (1, 2, 3):
        arrived(f"f_z{d}", fin.at[d - 1])
        total += fin[d - 1].astype(F32)
    flow = total.astype(BF16)
    pre = jnp.dot(mixing[...], flow, preferred_element_type=F32)
    pre += jnp.dot(input_weight[...], features[...], preferred_element_type=F32)
    new_state[...] = jnp.tanh(pre).astype(BF16)
    arrived("b_z", bin_)
    back = (bsum[0].astype(F32) + bin_[...].astype(F32)).astype(BF16)
    pulled = lax.dot_general(mixing[...], back, (((0,), (0,)), ((), ())), preferred_element_type=F32)
    own = states[col].astype(F32)
    new_adjoint[...] = ((1.0 - own * own) * (pulled + cotangent[...].astype(F32))).astype(BF16)

    for copy in sent:
        copy.wait_send()
    assert len(names) <= COPIES


def per_device(state, adjoint, features, cotangent, mixing, input_weight, tiles, tile_rows, tile_cols, live_tiles):
    blocks = lax.axis_size("col")
    slab = tiles[0, 0]
    slots = slab.shape[0]
    hidden, nodes = state.shape
    table = slot_table(tile_rows[0, 0], tile_cols[0, 0], live_tiles[0, 0], blocks)
    vmem = pl.BlockSpec(memory_space=pltpu.VMEM)
    anywhere = pl.BlockSpec(memory_space=pl.ANY)
    block = (hidden, nodes)
    half = (hidden // 2, nodes)
    return pl.pallas_call(
        kernel,
        out_shape=(jax.ShapeDtypeStruct(block, BF16), jax.ShapeDtypeStruct(block, BF16)),
        in_specs=[
            pl.BlockSpec(memory_space=pltpu.SMEM),
            anywhere,
            anywhere,
            vmem,
            vmem,
            vmem,
            vmem,
            anywhere,
        ],
        out_specs=(vmem, vmem),
        scratch_shapes=[
            pltpu.VMEM((slots + 1, SIDE, SIDE), BF16),
            pltpu.VMEM((blocks * SIDE, blocks * SIDE), BF16),
            pltpu.VMEM((blocks, *block), BF16),
            pltpu.VMEM((blocks, *block), BF16),
            pltpu.VMEM((blocks, *block), BF16),
            pltpu.VMEM((2, blocks // 2, *block), BF16),
            pltpu.VMEM((4, *half), BF16),
            pltpu.VMEM((4, *half), BF16),
            pltpu.VMEM((4, *block), BF16),
            pltpu.VMEM((4, *block), BF16),
            pltpu.VMEM((4, *block), BF16),
            pltpu.VMEM((3, *block), BF16),
            pltpu.VMEM((blocks // 2, *block), BF16),
            pltpu.VMEM((2, *half), BF16),
            pltpu.VMEM((2, *half), BF16),
            pltpu.VMEM((2, *block), BF16),
            pltpu.VMEM((2, *block), BF16),
            pltpu.VMEM((2, *block), BF16),
            pltpu.VMEM(block, BF16),
            pltpu.SemaphoreType.DMA((3,)),
            pltpu.SemaphoreType.DMA((COPIES,)),
            pltpu.SemaphoreType.DMA((COPIES,)),
        ],
        compiler_params=pltpu.CompilerParams(
            collective_id=0, has_side_effects=True, vmem_limit_bytes=56 * 1024 * 1024
        ),
        name="joint_step",
    )(table, state, adjoint, features, cotangent, mixing, input_weight, slab)


def solution(mesh):
    placed = (
        P(None, ("row", "col")),
        P(None, ("col", "row")),
        P(None, ("col", "row")),
        P(None, ("row", "col")),
        P(),
        P(),
        P("row", "col", None, None, None),
        P("row", "col", None),
        P("row", "col", None),
        P("row", "col"),
    )
    return jax.shard_map(
        per_device,
        mesh=mesh,
        in_specs=placed,
        out_specs=(P(None, ("col", "row")), P(None, ("row", "col"))),
        check_vma=False,
    )
```

time: 223 us -> 60.6 us (0.27)
  waiting for transfers between devices: 60.4 us -> 0 us
  local copies, waits for them, and re-layouts: 58.4 us -> 2.95 us
  Pallas kernels: 0 us -> 54.3 us
  other arithmetic: 45.3 us -> 1.37 us
  matrix products: 28.9 us -> 0 us
  starting transfers between devices: 27.8 us -> 0 us
    all_to_all x4 -> x0, waiting for transfers between devices: 60.4 us -> none  [the longest x2 31.6 us: copy_for_each(): return lax.all_to_all(copies, axis, split_axis=0, concat_axis=0, tiled=True)]
    pallas_call x0 -> x1, Pallas kernels: none -> 54.3 us  [per_device(): pl.pallas_call(kernel, out_shape=(jax.ShapeDtypeStruct(block, BF16), jax....]
    scatter-add x6 -> x0, other arithmetic: 38.9 us -> none  [the longest x3 19.4 us: forward_part(): return total.at[:, slot_cols].add(terms * live[None, :, None])]
    mul x6 -> x0, local copies, waits for them, and re-layouts: 33.6 us -> none  [the longest x3 16.8 us: forward_part(): return total.at[:, slot_cols].add(terms * live[None, :, None])]
    dot_general x9 -> x0, matrix products: 28.9 us -> none  [the longest x3 14.3 us: forward_part(): jnp.einsum('hsk,skn->hsn', picked, slot_tiles, preferred_element_type=jnp...]
    all_to_all x4 -> x0, starting transfers between devices: 27.8 us -> none  [the longest x2 16.7 us: copy_for_each(): return lax.all_to_all(copies, axis, split_axis=0, concat_axis=0, tiled=True)]
    gather x6 -> x0, local copies, waits for them, and re-layouts: 16.5 us -> none  [the longest x3 10.1 us: forward_part(): picked = jnp.take(whole, slot_rows, axis=1)]
    and x6 -> x0, other arithmetic: 4.37 us -> none  [the longest x3 2.19 us: forward_part(): picked = jnp.take(whole, slot_rows, axis=1)]
  transfers between devices with their start and end apart: 4 -> 0, of which waited for: 2 -> 0; matrix products, arithmetic and copies ran while one was open for 58% -> 0% of each run, Pallas kernels for 0% -> 0%
where the time goes in v1:
time: 60.6 us; the launch traced here: 59.9 us
  Pallas kernels  54.3 us (90%)
  local copies, waits for them, and re-layouts  2.95 us (5%)
  other arithmetic  1.37 us (2%)
  between operations  1.29 us (2%)
    pallas_call x1, Pallas kernels, per_device(): pl.pallas_call(kernel, out_shape=(jax.ShapeDtypeStruct(block, BF16), jax....  54.3 us
    unnamed x2, local copies, waits for them, and re-layouts  2.95 us

profile of v1, /device:TPU:32, one launch (start us, length us, event | category | flops | bytes accessed | tf_op | source)
XLA Modules:
  0.0 59.9 jit_solution(17170851220989755392)
XLA Ops:
  1.3 0.7 %add_bitcast_fusion = s32[85]{0:T(128)S(1)} fusion(s32[1,1,85]{2,1,0:T(1,128)} %param.18, s32[1,1,85]{2,1,0:T(1,128)} %param.17), kind=kLoop, calls=%fused_computation.6 | loop fusion | flops 170 | bytes 1020 | tf_op jit(solution)/shard_map/add | solution.py:19
  2.0 0.1 select_reduce_fusion
  2.1 0.6 broadcast_add_fusion.slot_of
  2.7 54.3 %joint_step.1 = (bf16[256,128]{1,0:T(8,128)(2,1)}, bf16[256,128]{1,0:T(8,128)(2,1)}) custom-call(s32[256]{0:T(256)} %broadcast_add_fusion.slot_of, bf16[256,128]{1,0:T(8,128)(2,1)} %state_hbm.1, bf16[256,128]{1,0:T(8,128)(2,1)} %adjoint_hbm.1, bf16[128,128]{1,0:T(8,128)(2,1)} %features.1, bf16[256,128]{1,0:T(8,128)(2,1)} %cotangent.1, ...), custom_call_target="tpu_custom_call" | custom-call | tf_op jit(solution)/shard_map/joint_step/pallas_call | solution.py:297
  56.9 1.5 %copy.15 = bf16[256,128]{1,0:T(8,128)(2,1)} copy(bf16[256,128]{1,0:T(8,128)(2,1)} %get-tuple-element.4) | data formatting | bytes 131072
  58.4 1.5 %copy.16 = bf16[256,128]{1,0:T(8,128)(2,1)} copy(bf16[256,128]{1,0:T(8,128)(2,1)} %get-tuple-element.5) | data formatting | bytes 131072
  (2 shorter events, 0.0 us)

commit v2 on v1

v2 whole, which is shorter than its diff:
```python
import functools

import jax
import jax.numpy as jnp
from jax import lax
from jax.experimental import pallas as pl
from jax.experimental.pallas import tpu as pltpu
from jax.sharding import PartitionSpec as P

SIDE = 128
BF16 = jnp.bfloat16
F32 = jnp.float32
COPIES = 72


def kernel(
    tile_rows,
    tile_cols,
    live_tiles,
    state_hbm,
    adjoint_hbm,
    tiles_hbm,
    flow,
    back,
    tiles,
    dense,
    table,
    slot_of,
    states,
    adjoints,
    fpart,
    fhalf_up,
    fhalf_down,
    ffull_up,
    ffull_down,
    ftotal,
    fsum,
    fin,
    bpart,
    bcore,
    bring,
    btotal,
    bsum,
    bin_,
    local_sems,
    send_sems,
    recv_sems,
):
    row = lax.axis_index("row")
    col = lax.axis_index("col")
    x, zl = row // 4, row % 4
    y, zh, core = col // 4, (col // 2) % 2, col % 2
    slots = tiles_hbm.shape[0]
    blocks = dense.shape[0] // SIDE

    def row_of(dx, dz):
        return ((x + dx) % 4) * 4 + (zl + dz) % 4

    def col_of(dy, dh, dk):
        return ((y + dy) % 4) * 4 + ((zh + dh) % 2) * 2 + (core + dk) % 2

    def to_row(dx, dz):
        return {"row": row_of(dx, dz), "col": col}

    def to_col(dy, dh, dk):
        return {"row": row, "col": col_of(dy, dh, dk)}

    partners = [to_col(0, 1, 0), to_row(0, 1), to_row(0, 2), to_row(0, 3)]
    partners += [to_col(2, 0, 0), to_col(1, 0, 0), to_col(3, 0, 0), to_row(1, 0), to_row(3, 0), to_col(0, 0, 1)]
    barrier = pltpu.get_barrier_semaphore()
    for partner in partners:
        pl.semaphore_signal(barrier, inc=1, device_id=partner, device_id_type=pl.DeviceIdType.MESH)

    end = (zl == 0) | (zl == 3)
    near = [
        jnp.where(zl == 0, 3, 1),
        jnp.where(end, 2, 3),
        jnp.where(zl == 0, 1, jnp.where(zl == 3, 3, 2)),
    ]

    sent = []
    names = {}
    used = [0]

    def number(name, count=1):
        if name not in names:
            names[name] = used[0]
            used[0] += count
        return names[name]

    def send(name, src, dst, device, which=0, count=1):
        n = number(name, count) + which
        copy = pltpu.make_async_remote_copy(
            src_ref=src,
            dst_ref=dst,
            send_sem=send_sems.at[n],
            recv_sem=recv_sems.at[n],
            device_id=device,
            device_id_type=pl.DeviceIdType.MESH,
        )
        copy.start()
        sent.append(copy)

    def arrived(name, ref, which=0):
        n = names[name] + which
        pltpu.make_async_remote_copy(
            src_ref=ref,
            dst_ref=ref,
            send_sem=send_sems.at[n],
            recv_sem=recv_sems.at[n],
            device_id=partners[0],
            device_id_type=pl.DeviceIdType.MESH,
        ).wait_recv()

    upper, lower = pl.ds(0, 128), pl.ds(128, 128)

    state_copy = pltpu.make_async_copy(state_hbm, states.at[col], local_sems.at[0])
    adjoint_copy = pltpu.make_async_copy(adjoint_hbm, adjoints.at[row], local_sems.at[1])
    tile_copy = pltpu.make_async_copy(tiles_hbm, tiles.at[pl.ds(0, slots)], local_sems.at[2])
    state_copy.start()
    adjoint_copy.start()
    tile_copy.start()
    tiles[slots] = jnp.zeros((SIDE, SIDE), BF16)

    places = tile_rows[...] * blocks + tile_cols[...]
    across = lax.broadcasted_iota(jnp.int32, (slots, slots), 1)
    down = lax.broadcasted_iota(jnp.int32, (slots, slots), 0)
    places = jnp.sum(jnp.where(across == down, jnp.broadcast_to(places, (slots, slots)), 0), axis=1, keepdims=True)
    ids = lax.broadcasted_iota(jnp.int32, (slots, SIDE), 0)
    for part in range(blocks * blocks // SIDE):
        here = (places == lax.broadcasted_iota(jnp.int32, (slots, SIDE), 1) + part * SIDE) & (ids < live_tiles[0, 0])
        found = jnp.sum(jnp.where(here, ids - slots, 0), axis=0, keepdims=True)
        table[part : part + 1] = found + slots
    table_copy = pltpu.make_async_copy(table, slot_of, local_sems.at[3])
    table_copy.start()
    state_copy.wait()
    adjoint_copy.wait()
    pl.semaphore_wait(barrier, len(partners))

    own_state, own_adjoint = states.at[col], adjoints.at[row]
    send("s_z", own_state, own_state, to_col(0, 1, 0))
    send("a_z", own_adjoint, own_adjoint, to_row(0, 4 - near[0]), 4 - near[0], 4)
    send("a_up0", own_adjoint, own_adjoint, to_row(1, 0))
    send("a_dn0", own_adjoint, own_adjoint, to_row(3, 0))
    send("a_z", own_adjoint, own_adjoint, to_row(0, 4 - near[1]), 4 - near[1], 4)
    send("a_z", own_adjoint, own_adjoint, to_row(0, 4 - near[2]), 4 - near[2], 4)
    for dy in (2, 1, 3):
        send(f"s_y{dy}0", own_state, own_state, to_col(dy, 0, 0))
    send("s_k00", own_state, own_state, to_col(0, 0, 1))

    tile_copy.wait()
    table_copy.wait()

    def place(r, carry):
        start = pl.multiple_of(r * SIDE, SIDE)
        for c in range(blocks):
            n = r * blocks + c
            dense[pl.ds(start, SIDE), c * SIDE : (c + 1) * SIDE] = tiles[slot_of[n // SIDE, n % SIDE]]
        return carry

    lax.fori_loop(0, blocks, place, 0)

    def adjoint_onward(i):
        block = adjoints.at[row_of(0, 4 - near[i])]
        arrived("a_z", block, near[i])
        send(f"a_up{i + 1}", block, block, to_row(1, 0))
        send(f"a_dn{i + 1}", block, block, to_row(3, 0))

    def adjoint_far(i):
        dz = 4 - near[i - 1] if i else 0
        block = adjoints.at[row_of(3, dz)]
        arrived(f"a_up{i}", block)
        send(f"a_far_up{i}", block.at[upper], block.at[upper], to_row(1, 0))
        block = adjoints.at[row_of(1, dz)]
        arrived(f"a_dn{i}", block)
        send(f"a_far_dn{i}", block.at[lower], block.at[lower], to_row(3, 0))

    adjoint_onward(0)
    adjoint_far(0)
    block = states.at[col_of(0, 1, 0)]
    arrived("s_z", block)
    for dy in (2, 1, 3):
        send(f"s_y{dy}1", block, block, to_col(dy, 0, 0))
    send("s_k01", block, block, to_col(0, 0, 1))
    adjoint_onward(1)
    adjoint_far(1)
    for dy in (1, 3, 2):
        block = states.at[col_of(4 - dy, 0, 0)]
        arrived(f"s_y{dy}0", block)
        send(f"s_k{dy}0", block, block, to_col(0, 0, 1))
    adjoint_onward(2)
    adjoint_far(2)
    for dy in (1, 3, 2):
        block = states.at[col_of(4 - dy, 1, 0)]
        arrived(f"s_y{dy}1", block)
        send(f"s_k{dy}1", block, block, to_col(0, 0, 1))
    adjoint_far(3)
    for h in (0, 1):
        for dy in (0, 1, 3, 2):
            arrived(f"s_k{dy}{h}", states.at[col_of(4 - dy, h, 1)])

    def forward(dx):
        first = ((x + dx) % 4) * 4
        whole = jnp.concatenate([states[i] for i in range(blocks)], axis=1)
        start = pl.multiple_of(first * SIDE, SIDE)
        product = jnp.dot(whole, dense[:, pl.ds(start, 4 * SIDE)], preferred_element_type=F32)
        for i in range(4):
            fpart[first + i] = product[:, i * SIDE : (i + 1) * SIDE].astype(BF16)

    zorder = [4 - near[2], 4 - near[1], 4 - near[0], 0]

    forward(2)
    for i, dz in enumerate(zorder):
        block = fpart.at[row_of(2, dz)]
        send(f"f_half_up{i}", block.at[upper], fhalf_up.at[i], to_row(1, 0))
        send(f"f_half_dn{i}", block.at[lower], fhalf_down.at[i], to_row(3, 0))
    forward(1)
    forward(3)
    for i, dz in enumerate(zorder):
        block = fpart.at[row_of(1, dz)]
        arrived(f"f_half_up{i}", fhalf_up.at[i])
        block[0:128] = (block[0:128].astype(F32) + fhalf_up[i].astype(F32)).astype(BF16)
        send(f"f_full_up{i}", block, ffull_up.at[i], to_row(1, 0))
        block = fpart.at[row_of(3, dz)]
        arrived(f"f_half_dn{i}", fhalf_down.at[i])
        block[128:256] = (block[128:256].astype(F32) + fhalf_down[i].astype(F32)).astype(BF16)
        send(f"f_full_dn{i}", block, ffull_down.at[i], to_row(3, 0))
    forward(0)

    for i in range(4):
        block = adjoints.at[row_of(2, 4 - near[i - 1] if i else 0)]
        arrived(f"a_far_up{i}", block.at[upper])
        arrived(f"a_far_dn{i}", block.at[lower])

    def backward(dy):
        first = ((y + dy) % 4) * 4
        whole = jnp.concatenate([adjoints[i] for i in range(blocks)], axis=1)
        start = pl.multiple_of(first * SIDE, SIDE)
        product = lax.dot_general(
            whole, dense[pl.ds(start, 4 * SIDE), :], (((1,), (1,)), ((), ())), preferred_element_type=F32
        )
        for i in range(4):
            bpart[i % 2, first // 2 + i // 2] = product[:, i * SIDE : (i + 1) * SIDE].astype(BF16)

    for dy in (2, 1, 3, 0):
        backward(dy)
        pair = pl.ds(((y + dy) % 4) * 2, 2)
        send(f"b_k{dy}", bpart.at[1 - core, pair], bcore.at[pair], to_col(0, 0, 1))

    for dy in (2, 1, 3, 0):
        first = ((y + dy) % 4) * 2
        pair = pl.ds(first, 2)
        arrived(f"b_k{dy}", bcore.at[pair])
        if dy:
            for i in range(2):
                bcore[first + i] = (bcore[first + i].astype(F32) + bpart[core, first + i].astype(F32)).astype(BF16)
            send(f"b_y{dy}", bcore.at[pair], bring.at[dy - 1], to_col(dy, 0, 0))

    def forward_sum(i):
        arrived(f"f_full_up{i}", ffull_up.at[i])
        arrived(f"f_full_dn{i}", ffull_down.at[i])
        dz = zorder[i]
        total = fpart[row_of(0, dz)].astype(F32) + ffull_up[i].astype(F32) + ffull_down[i].astype(F32)
        if i < 3:
            fsum[i] = total.astype(BF16)
            send("f_z", fsum.at[i], fin.at[dz - 1], to_row(0, dz), dz, 4)
        else:
            ftotal[...] = total

    forward_sum(0)
    forward_sum(1)
    for dy in (1, 3, 2):
        arrived(f"b_y{dy}", bring.at[dy - 1])
    for h in (1, 0):
        n = (zh + h) % 2
        total = bcore[y * 2 + n].astype(F32) + bpart[core, y * 2 + n].astype(F32)
        for dy in (1, 2, 3):
            total += bring[dy - 1, n].astype(F32)
        if h:
            bsum[...] = total.astype(BF16)
            send("b_z", bsum, bin_, to_col(0, 1, 0))
        else:
            btotal[...] = total
    forward_sum(2)
    forward_sum(3)

    total = ftotal[...]
    for d in (1, 2, 3):
        arrived("f_z", fin.at[d - 1], d)
        total += fin[d - 1].astype(F32)
    flow[...] = total.astype(BF16)
    arrived("b_z", bin_)
    back[...] = (btotal[...] + bin_[...].astype(F32)).astype(BF16)

    for copy in sent:
        copy.wait_send()
    assert used[0] <= COPIES


def per_device(state, adjoint, features, cotangent, mixing, input_weight, tiles, tile_rows, tile_cols, live_tiles):
    blocks = lax.axis_size("col")
    slab = tiles[0, 0]
    slots = slab.shape[0]
    hidden, nodes = state.shape
    vmem = pl.BlockSpec(memory_space=pltpu.VMEM)
    smem = pl.BlockSpec(memory_space=pltpu.SMEM)
    anywhere = pl.BlockSpec(memory_space=pl.ANY)
    block = (hidden, nodes)
    half = (hidden // 2, nodes)
    flow, back = pl.pallas_call(
        kernel,
        out_shape=(jax.ShapeDtypeStruct(block, BF16), jax.ShapeDtypeStruct(block, BF16)),
        in_specs=[vmem, vmem, smem, anywhere, anywhere, anywhere],
        out_specs=(vmem, vmem),
        scratch_shapes=[
            pltpu.VMEM((slots + 1, SIDE, SIDE), BF16),
            pltpu.VMEM((blocks * SIDE, blocks * SIDE), BF16),
            pltpu.VMEM((blocks * blocks // SIDE, SIDE), jnp.int32),
            pltpu.SMEM((blocks * blocks // SIDE, SIDE), jnp.int32),
            pltpu.VMEM((blocks, *block), BF16),
            pltpu.VMEM((blocks, *block), BF16),
            pltpu.VMEM((blocks, *block), BF16),
            pltpu.VMEM((4, *half), BF16),
            pltpu.VMEM((4, *half), BF16),
            pltpu.VMEM((4, *block), BF16),
            pltpu.VMEM((4, *block), BF16),
            pltpu.VMEM(block, F32),
            pltpu.VMEM((3, *block), BF16),
            pltpu.VMEM((3, *block), BF16),
            pltpu.VMEM((2, blocks // 2, *block), BF16),
            pltpu.VMEM((blocks // 2, *block), BF16),
            pltpu.VMEM((3, 2, *block), BF16),
            pltpu.VMEM(block, F32),
            pltpu.VMEM(block, BF16),
            pltpu.VMEM(block, BF16),
            pltpu.SemaphoreType.DMA((4,)),
            pltpu.SemaphoreType.DMA((COPIES,)),
            pltpu.SemaphoreType.DMA((COPIES,)),
        ],
        compiler_params=pltpu.CompilerParams(
            collective_id=0, has_side_effects=True, vmem_limit_bytes=56 * 1024 * 1024
        ),
        name="joint_step",
    )(tile_rows[0], tile_cols[0], live_tiles, state, adjoint, slab)
    pre = jnp.dot(mixing, flow, preferred_element_type=F32)
    pre = pre + jnp.dot(input_weight, features, preferred_element_type=F32)
    new_state = jnp.tanh(pre).astype(BF16)
    pulled = jnp.dot(mixing.T, back, preferred_element_type=F32)
    wide = state.astype(F32)
    new_adjoint = ((1.0 - wide * wide) * (pulled + cotangent.astype(F32))).astype(BF16)
    return new_state, new_adjoint


def solution(mesh):
    placed = (
        P(None, ("row", "col")),
        P(None, ("col", "row")),
        P(None, ("col", "row")),
        P(None, ("row", "col")),
        P(),
        P(),
        P("row", "col", None, None, None),
        P("row", "col", None),
        P("row", "col", None),
        P("row", "col"),
    )
    return jax.shard_map(
        per_device,
        mesh=mesh,
        in_specs=placed,
        out_specs=(P(None, ("col", "row")), P(None, ("row", "col"))),
        check_vma=False,
    )
```

time: 60.6 us -> 59.1 us (0.975)
  Pallas kernels: 54.3 us -> 51.6 us
  matrix products: 0 us -> 2.3 us
  other arithmetic: 1.37 us -> 0 us
    pallas_call x1, Pallas kernels: 54.3 us -> 51.6 us  [per_device(): pl.pallas_call(kernel, out_shape=(jax.ShapeDtypeStruct(block, BF16), jax....]
    dot_general x0 -> x3, matrix products: none -> 2.3 us  [the longest x1 1.05 us: per_device(): pre = jnp.dot(mixing, flow, preferred_element_type=F32)]
    add x2 -> x0, other arithmetic: 1.25 us -> none  [the longest x1 0.68 us: slot_table(): places = rows * blocks + cols]
    unnamed x2 -> x10, local copies, waits for them, and re-layouts: 2.95 us -> 3.37 us
where the time goes in v2:
time: 59.1 us; the launch traced here: 58.6 us
  Pallas kernels  51.6 us (87%)
  local copies, waits for them, and re-layouts  3.37 us (6%)
  matrix products  2.3 us (4%)
  between operations  1.38 us (2%)
    pallas_call x1, Pallas kernels, per_device(): pl.pallas_call(kernel, out_shape=(jax.ShapeDtypeStruct(block, BF16), jax....  51.6 us
    unnamed x10, local copies, waits for them, and re-layouts  3.37 us

profile of v2, /device:TPU:32, one launch (start us, length us, event | category | flops | bytes accessed | tf_op | source)
XLA Modules:
  0.0 58.6 jit_solution(8915512314454560400)
XLA Ops:
  0.6 0.0 copy-start
  0.6 0.0 copy-start.1
  0.7 0.0 copy-start.2
  1.3 0.9 %copy.14 = bf16[256,128]{0,1:T(8,128)(2,1)S(1)} copy(bf16[256,128]{1,0:T(8,128)(2,1)} %param.13) | data formatting | bytes 131072 | tf_op args[3]
  2.3 0.9 %copy.13 = bf16[256,128]{0,1:T(8,128)(2,1)S(1)} copy(bf16[256,128]{1,0:T(8,128)(2,1)} %state_hbm.1) | data formatting | bytes 131072 | tf_op args[0]
  3.2 51.6 %joint_step.1 = (bf16[256,128]{1,0:T(8,128)(2,1)}, bf16[256,128]{1,0:T(8,128)(2,1)}) custom-call(s32[1,85]{1,0:T(1,128)} %bitcast.26, s32[1,85]{1,0:T(1,128)} %bitcast.27, s32[1,1]{1,0:T(1,128)S(6)} %copy.18.live_tiles, bf16[256,128]{1,0:T(8,128)(2,1)} %state_hbm.1, bf16[256,128]{1,0:T(8,128)(2,1)} %adjoint_hbm.1, bf16[85,128,128]{2,1,0:T(8,128)(2,1)} %bitcast.25), custom_call_target="tpu_custom_call" | custom-call | tf_op jit(solution)/shard_map/joint_step/pallas_call | solution.py:310
  54.8 0.0 copy-done
  54.8 1.0 %fusion.4 = bf16[256,128]{0,1:T(8,128)(2,1)S(1)} fusion(bf16[256,128]{1,0:T(8,128)(2,1)} %get-tuple-element.5, bf16[256,256]{1,0:T(8,128)(2,1)S(1)} %copy-done, bf16[256,128]{0,1:T(8,128)(2,1)S(1)} %copy.14, bf16[256,128]{0,1:T(8,128)(2,1)S(1)} %copy.13), kind=kOutput, calls=%fused_computation.6 | convolution fusion | flops 17006592 | bytes 393216 | tf_op jit(solution)/shard_map/dot_general | solution.py:348
  55.8 0.7 %copy.16 = bf16[256,128]{1,0:T(8,128)(2,1)} copy(bf16[256,128]{0,1:T(8,128)(2,1)S(1)} %fusion.4) | data formatting | bytes 131072
  56.6 0.0 copy-done.1
  56.6 0.0 copy-done.2
  56.6 0.2 fusion.6
  56.8 1.0 %fusion.5 = bf16[256,128]{0,1:T(8,128)(2,1)S(1)} fusion(f32[256,128]{0,1:T(8,128)S(1)} %fusion.6, bf16[256,128]{1,0:T(8,128)(2,1)} %get-tuple-element.4, bf16[256,256]{1,0:T(8,128)(2,1)S(1)} %copy-done), kind=kOutput, calls=%fused_computation.7 | convolution fusion | flops 16842752 | bytes 393216 | tf_op jit(solution)/shard_map/dot_general | solution.py:345
  57.9 0.7 %copy.15 = bf16[256,128]{1,0:T(8,128)(2,1)} copy(bf16[256,128]{0,1:T(8,128)(2,1)S(1)} %fusion.5) | data formatting | bytes 131072
Async XLA Ops:
  0.6 54.2 %copy-start = (bf16[256,256]{1,0:T(8,128)(2,1)S(1)}, bf16[256,256]{1,0:T(8,128)(2,1)}, u32[]{:S(2)}) copy-start(bf16[256,256]{1,0:T(8,128)(2,1)} %param.14) | copy-start | bytes 393220
  0.6 55.9 %copy-start.1 = (bf16[256,128]{1,0:T(8,128)(2,1)S(1)}, bf16[256,128]{1,0:T(8,128)(2,1)}, u32[]{:S(2)}) copy-start(bf16[256,128]{1,0:T(8,128)(2,1)} %param.15) | copy-start | bytes 196612
  0.7 55.9 %copy-start.2 = (bf16[128,128]{1,0:T(8,128)(2,1)S(1)}, bf16[128,128]{1,0:T(8,128)(2,1)}, u32[]{:S(2)}) copy-start(bf16[128,128]{1,0:T(8,128)(2,1)} %param.12) | copy-start | bytes 98308

commit v3 on v2

--- a/solution.py
+++ b/solution.py
@@ -14,14 +14,24 @@
 
 
 def kernel(
+    state_hbm,
+    adjoint_hbm,
+    tiles_hbm,
+    tile_rows_hbm,
+    tile_cols_hbm,
+    live_tiles_hbm,
+    features_hbm,
+    cotangent_hbm,
+    mixing_hbm,
+    input_weight_hbm,
+    result,
     tile_rows,
     tile_cols,
     live_tiles,
-    state_hbm,
-    adjoint_hbm,
-    tiles_hbm,
-    flow,
-    back,
+    features,
+    cotangent,
+    mixing,
+    input_weight,
     tiles,
     dense,
     table,
@@ -114,13 +124,29 @@
 
     upper, lower = pl.ds(0, 128), pl.ds(128, 128)
 
-    state_copy = pltpu.make_async_copy(state_hbm, states.at[col], local_sems.at[0])
-    adjoint_copy = pltpu.make_async_copy(adjoint_hbm, adjoints.at[row], local_sems.at[1])
-    tile_copy = pltpu.make_async_copy(tiles_hbm, tiles.at[pl.ds(0, slots)], local_sems.at[2])
-    state_copy.start()
-    adjoint_copy.start()
-    tile_copy.start()
+    def fetch(src, dst, n):
+        copy = pltpu.make_async_copy(src, dst, local_sems.at[n])
+        copy.start()
+        return copy
+
+    index_copies = [
+        fetch(tile_rows_hbm, tile_rows, 4),
+        fetch(tile_cols_hbm, tile_cols, 5),
+        fetch(live_tiles_hbm, live_tiles, 6),
+    ]
+    state_copy = fetch(state_hbm, states.at[col], 0)
+    adjoint_copy = fetch(adjoint_hbm, adjoints.at[row], 1)
+    tile_copy = fetch(tiles_hbm, tiles.at[pl.ds(0, slots)], 2)
+    late_copies = [
+        fetch(features_hbm, features, 7),
+        fetch(cotangent_hbm, cotangent, 8),
+        fetch(mixing_hbm, mixing, 9),
+        fetch(input_weight_hbm, input_weight, 10),
+    ]
     tiles[slots] = jnp.zeros((SIDE, SIDE), BF16)
+
+    for copy in index_copies:
+        copy.wait()
 
     places = tile_rows[...] * blocks + tile_cols[...]
     across = lax.broadcasted_iota(jnp.int32, (slots, slots), 1)
@@ -175,26 +201,25 @@
         arrived(f"a_dn{i}", block)
         send(f"a_far_dn{i}", block.at[lower], block.at[lower], to_row(3, 0))
 
+    def states_over(h):
+        for dy in (1, 3, 2):
+            block = states.at[col_of(4 - dy, h, 0)]
+            arrived(f"s_y{dy}{h}", block)
+            send(f"s_k{dy}{h}", block, block, to_col(0, 0, 1))
+
+    adjoint_far(0)
     adjoint_onward(0)
-    adjoint_far(0)
     block = states.at[col_of(0, 1, 0)]
     arrived("s_z", block)
     for dy in (2, 1, 3):
         send(f"s_y{dy}1", block, block, to_col(dy, 0, 0))
     send("s_k01", block, block, to_col(0, 0, 1))
     adjoint_onward(1)
+    states_over(0)
+    adjoint_onward(2)
     adjoint_far(1)
-    for dy in (1, 3, 2):
-        block = states.at[col_of(4 - dy, 0, 0)]
-        arrived(f"s_y{dy}0", block)
-        send(f"s_k{dy}0", block, block, to_col(0, 0, 1))
-    adjoint_onward(2)
+    states_over(1)
     adjoint_far(2)
-    for dy in (1, 3, 2):
-        block = states.at[col_of(4 - dy, 1, 0)]
-        arrived(f"s_y{dy}1", block)
-        send(f"s_k{dy}1", block, block, to_col(0, 0, 1))
-    adjoint_far(3)
     for h in (0, 1):
         for dy in (0, 1, 3, 2):
             arrived(f"s_k{dy}{h}", states.at[col_of(4 - dy, h, 1)])
@@ -208,29 +233,6 @@
             fpart[first + i] = product[:, i * SIDE : (i + 1) * SIDE].astype(BF16)
 
     zorder = [4 - near[2], 4 - near[1], 4 - near[0], 0]
-
-    forward(2)
-    for i, dz in enumerate(zorder):
-        block = fpart.at[row_of(2, dz)]
-        send(f"f_half_up{i}", block.at[upper], fhalf_up.at[i], to_row(1, 0))
-        send(f"f_half_dn{i}", block.at[lower], fhalf_down.at[i], to_row(3, 0))
-    forward(1)
-    forward(3)
-    for i, dz in enumerate(zorder):
-        block = fpart.at[row_of(1, dz)]
-        arrived(f"f_half_up{i}", fhalf_up.at[i])
-        block[0:128] = (block[0:128].astype(F32) + fhalf_up[i].astype(F32)).astype(BF16)
-        send(f"f_full_up{i}", block, ffull_up.at[i], to_row(1, 0))
-        block = fpart.at[row_of(3, dz)]
-        arrived(f"f_half_dn{i}", fhalf_down.at[i])
-        block[128:256] = (block[128:256].astype(F32) + fhalf_down[i].astype(F32)).astype(BF16)
-        send(f"f_full_dn{i}", block, ffull_down.at[i], to_row(3, 0))
-    forward(0)
-
-    for i in range(4):
-        block = adjoints.at[row_of(2, 4 - near[i - 1] if i else 0)]
-        arrived(f"a_far_up{i}", block.at[upper])
-        arrived(f"a_far_dn{i}", block.at[lower])
 
     def backward(dy):
         first = ((y + dy) % 4) * 4
@@ -241,20 +243,53 @@
         )
         for i in range(4):
             bpart[i % 2, first // 2 + i // 2] = product[:, i * SIDE : (i + 1) * SIDE].astype(BF16)
-
-    for dy in (2, 1, 3, 0):
-        backward(dy)
         pair = pl.ds(((y + dy) % 4) * 2, 2)
         send(f"b_k{dy}", bpart.at[1 - core, pair], bcore.at[pair], to_col(0, 0, 1))
 
-    for dy in (2, 1, 3, 0):
+    def over_cores(dy):
         first = ((y + dy) % 4) * 2
         pair = pl.ds(first, 2)
         arrived(f"b_k{dy}", bcore.at[pair])
-        if dy:
-            for i in range(2):
-                bcore[first + i] = (bcore[first + i].astype(F32) + bpart[core, first + i].astype(F32)).astype(BF16)
-            send(f"b_y{dy}", bcore.at[pair], bring.at[dy - 1], to_col(dy, 0, 0))
+        for i in range(2):
+            bcore[first + i] = (bcore[first + i].astype(F32) + bpart[core, first + i].astype(F32)).astype(BF16)
+        send(f"b_y{dy}", bcore.at[pair], bring.at[dy - 1], to_col(dy, 0, 0))
+
+    def near_sum(i):
+        dz = zorder[i]
+        block = fpart.at[row_of(1, dz)]
+        arrived(f"f_half_up{i}", fhalf_up.at[i])
+        block[0:128] = (block[0:128].astype(F32) + fhalf_up[i].astype(F32)).astype(BF16)
+        send(f"f_full_up{i}", block, ffull_up.at[i], to_row(1, 0))
+        block = fpart.at[row_of(3, dz)]
+        arrived(f"f_half_dn{i}", fhalf_down.at[i])
+        block[128:256] = (block[128:256].astype(F32) + fhalf_down[i].astype(F32)).astype(BF16)
+        send(f"f_full_dn{i}", block, ffull_down.at[i], to_row(3, 0))
+
+    forward(2)
+    for i, dz in enumerate(zorder):
+        block = fpart.at[row_of(2, dz)]
+        send(f"f_half_up{i}", block.at[upper], fhalf_up.at[i], to_row(1, 0))
+        send(f"f_half_dn{i}", block.at[lower], fhalf_down.at[i], to_row(3, 0))
+    adjoint_far(3)
+    forward(1)
+    forward(3)
+    near_sum(0)
+    near_sum(1)
+
+    for i in range(4):
+        block = adjoints.at[row_of(2, 4 - near[i - 1] if i else 0)]
+        arrived(f"a_far_up{i}", block.at[upper])
+        arrived(f"a_far_dn{i}", block.at[lower])
+    backward(2)
+    near_sum(2)
+    near_sum(3)
+    backward(1)
+    over_cores(2)
+    backward(3)
+    over_cores(1)
+    forward(0)
+    over_cores(3)
+    backward(0)
 
     def forward_sum(i):
         arrived(f"f_full_up{i}", ffull_up.at[i])
@@ -269,11 +304,13 @@
 
     forward_sum(0)
     forward_sum(1)
+    first = y * 2
+    arrived("b_k0", bcore.at[pl.ds(first, 2)])
     for dy in (1, 3, 2):
         arrived(f"b_y{dy}", bring.at[dy - 1])
     for h in (1, 0):
         n = (zh + h) % 2
-        total = bcore[y * 2 + n].astype(F32) + bpart[core, y * 2 + n].astype(F32)
+        total = bcore[first + n].astype(F32) + bpart[core, first + n].astype(F32)
         for dy in (1, 2, 3):
             total += bring[dy - 1, n].astype(F32)
         if h:
@@ -284,13 +321,18 @@
     forward_sum(2)
     forward_sum(3)
 
+    for copy in late_copies:
+        copy.wait()
+    fed = jnp.dot(input_weight[...], features[...], preferred_element_type=F32)
     total = ftotal[...]
     for d in (1, 2, 3):
         arrived("f_z", fin.at[d - 1], d)
         total += fin[d - 1].astype(F32)
-    flow[...] = total.astype(BF16)
+    result[0] = fed + jnp.dot(mixing[...], total.astype(BF16), preferred_element_type=F32)
     arrived("b_z", bin_)
-    back[...] = (btotal[...] + bin_[...].astype(F32)).astype(BF16)
+    back = (btotal[...] + bin_[...].astype(F32)).astype(BF16)
+    pulled = lax.dot_general(mixing[...], back, (((0,), (0,)), ((), ())), preferred_element_type=F32)
+    result[1] = pulled + cotangent[...].astype(F32)
 
     for copy in sent:
         copy.wait_send()
@@ -303,16 +345,22 @@
     slots = slab.shape[0]
     hidden, nodes = state.shape
     vmem = pl.BlockSpec(memory_space=pltpu.VMEM)
-    smem = pl.BlockSpec(memory_space=pltpu.SMEM)
     anywhere = pl.BlockSpec(memory_space=pl.ANY)
     block = (hidden, nodes)
     half = (hidden // 2, nodes)
-    flow, back = pl.pallas_call(
+    result = pl.pallas_call(
         kernel,
-        out_shape=(jax.ShapeDtypeStruct(block, BF16), jax.ShapeDtypeStruct(block, BF16)),
-        in_specs=[vmem, vmem, smem, anywhere, anywhere, anywhere],
-        out_specs=(vmem, vmem),
+        out_shape=jax.ShapeDtypeStruct((2, *block), F32),
+        in_specs=[anywhere] * 10,
+        out_specs=vmem,
         scratch_shapes=[
+            pltpu.VMEM((1, slots), jnp.int32),
+            pltpu.VMEM((1, slots), jnp.int32),
+            pltpu.SMEM((1, 1), jnp.int32),
+            pltpu.VMEM(features.shape, BF16),
+            pltpu.VMEM(block, BF16),
+            pltpu.VMEM(mixing.shape, BF16),
+            pltpu.VMEM(input_weight.shape, BF16),
             pltpu.VMEM((slots + 1, SIDE, SIDE), BF16),
             pltpu.VMEM((blocks * SIDE, blocks * SIDE), BF16),
             pltpu.VMEM((blocks * blocks // SIDE, SIDE), jnp.int32),
@@ -333,7 +381,7 @@
             pltpu.VMEM(block, F32),
             pltpu.VMEM(block, BF16),
             pltpu.VMEM(block, BF16),
-            pltpu.SemaphoreType.DMA((4,)),
+            pltpu.SemaphoreType.DMA((11,)),
             pltpu.SemaphoreType.DMA((COPIES,)),
             pltpu.SemaphoreType.DMA((COPIES,)),
         ],
@@ -341,13 +389,21 @@
             collective_id=0, has_side_effects=True, vmem_limit_bytes=56 * 1024 * 1024
         ),
         name="joint_step",
-    )(tile_rows[0], tile_cols[0], live_tiles, state, adjoint, slab)
-    pre = jnp.dot(mixing, flow, preferred_element_type=F32)
-    pre = pre + jnp.dot(input_weight, features, preferred_element_type=F32)
-    new_state = jnp.tanh(pre).astype(BF16)
-    pulled = jnp.dot(mixing.T, back, preferred_element_type=F32)
+    )(
+        state,
+        adjoint,
+        slab,
+        tile_rows[0],
+        tile_cols[0],
+        live_tiles,
+        features,
+        cotangent,
+        mixing,
+        input_weight,
+    )
+    new_state = jnp.tanh(result[0]).astype(BF16)
     wide = state.astype(F32)
-    new_adjoint = ((1.0 - wide * wide) * (pulled + cotangent.astype(F32))).astype(BF16)
+    new_adjoint = ((1.0 - wide * wide) * result[1]).astype(BF16)
     return new_state, new_adjoint
 
 

time: 59.1 us -> 54.1 us (0.915)
  local copies, waits for them, and re-layouts: 3.37 us -> 0.01 us
  other arithmetic: 0 us -> 3.11 us
  Pallas kernels: 51.6 us -> 49.3 us
  matrix products: 2.3 us -> 0 us
    unnamed x10 -> x2, local copies, waits for them, and re-layouts: 3.37 us -> 0.01 us
    convert_element_type x0 -> x2, other arithmetic: none -> 3.11 us  [the longest x1 1.56 us: per_device(): new_adjoint = ((1.0 - wide * wide) * result[1]).astype(BF16)]
    dot_general x3 -> x0, matrix products: 2.3 us -> none  [the longest x1 1.05 us: per_device(): pre = jnp.dot(mixing, flow, preferred_element_type=F32)]
    pallas_call x1, Pallas kernels: 51.6 us -> 49.3 us  [per_device(): pl.pallas_call(kernel, out_shape=jax.ShapeDtypeStruct((2, *block), F32),...]
where the time goes in v3:
time: 54.1 us; the launch traced here: 53.7 us
  Pallas kernels  49.3 us (91%)
  other arithmetic  3.11 us (6%)
  between operations  1.33 us (2%)
    pallas_call x1, Pallas kernels, per_device(): pl.pallas_call(kernel, out_shape=jax.ShapeDtypeStruct((2, *block), F32),...  49.3 us
    convert_element_type x1, other arithmetic, per_device(): new_adjoint = ((1.0 - wide * wide) * result[1]).astype(BF16)  1.56 us
    convert_element_type x1, other arithmetic, per_device(): new_state = jnp.tanh(result[0]).astype(BF16)  1.56 us

profile of v3, /device:TPU:32, one launch (start us, length us, event | category | flops | bytes accessed | tf_op | source)
XLA Modules:
  0.0 53.7 jit_solution(2310925226496464161)
XLA Ops:
  0.6 0.0 copy-start
  1.3 49.3 %joint_step.1 = f32[2,256,128]{2,1,0:T(8,128)} custom-call(bf16[256,128]{1,0:T(8,128)(2,1)} %state_hbm.1, bf16[256,128]{1,0:T(8,128)(2,1)} %adjoint_hbm.1, bf16[85,128,128]{2,1,0:T(8,128)(2,1)} %bitcast.9, s32[1,85]{1,0:T(1,128)} %bitcast.10, s32[1,85]{1,0:T(1,128)} %bitcast.11, s32[1,1]{1,0:T(1,128)S(6)} %copy.12.live_tiles_hbm, ...), custom_call_target="tpu_custom_call" | custom-call | tf_op jit(solution)/shard_map/joint_step/pallas_call | solution.py:351
  50.6 0.0 copy-done
  50.6 1.6 %fusion = bf16[256,128]{1,0:T(8,128)(2,1)} fusion(f32[2,256,128]{2,1,0:T(8,128)} %joint_step.1, bf16[256,128]{1,0:T(8,128)(2,1)S(1)} %copy-done), kind=kLoop, calls=%fused_computation.1 | loop fusion | flops 163840 | bytes 262144 | tf_op jit(solution)/shard_map/convert_element_type | solution.py:406
  52.2 1.6 %fusion.1 = bf16[256,128]{1,0:T(8,128)(2,1)} fusion(f32[2,256,128]{2,1,0:T(8,128)} %joint_step.1), kind=kLoop, calls=%fused_computation.3 | loop fusion | flops 32768 | bytes 196608 | tf_op jit(solution)/shard_map/convert_element_type | solution.py:404
Async XLA Ops:
  0.6 50.0 %copy-start = (bf16[256,128]{1,0:T(8,128)(2,1)S(1)}, bf16[256,128]{1,0:T(8,128)(2,1)}, u32[]{:S(2)}) copy-start(bf16[256,128]{1,0:T(8,128)(2,1)} %state_hbm.1) | copy-start | bytes 196612

commit v4 on v3

--- a/solution.py
+++ b/solution.py
@@ -10,7 +10,8 @@
 SIDE = 128
 BF16 = jnp.bfloat16
 F32 = jnp.float32
-COPIES = 72
+COPIES = 96
+STRAIGHT = (3,)
 
 
 def kernel(
@@ -24,7 +25,8 @@
     cotangent_hbm,
     mixing_hbm,
     input_weight_hbm,
-    result,
+    new_state,
+    new_adjoint,
     tile_rows,
     tile_cols,
     live_tiles,
@@ -76,7 +78,7 @@
         return {"row": row, "col": col_of(dy, dh, dk)}
 
     partners = [to_col(0, 1, 0), to_row(0, 1), to_row(0, 2), to_row(0, 3)]
-    partners += [to_col(2, 0, 0), to_col(1, 0, 0), to_col(3, 0, 0), to_row(1, 0), to_row(3, 0), to_col(0, 0, 1)]
+    partners += [to_row(2, 0), to_col(2, 0, 0), to_col(1, 0, 0), to_col(3, 0, 0), to_row(1, 0), to_row(3, 0), to_col(0, 0, 1)]
     barrier = pltpu.get_barrier_semaphore()
     for partner in partners:
         pl.semaphore_signal(barrier, inc=1, device_id=partner, device_id_type=pl.DeviceIdType.MESH)
@@ -189,6 +191,8 @@
     def adjoint_onward(i):
         block = adjoints.at[row_of(0, 4 - near[i])]
         arrived("a_z", block, near[i])
+        if i + 1 in STRAIGHT:
+            send(f"a_x2{i + 1}", block, block, to_row(2, 0))
         send(f"a_up{i + 1}", block, block, to_row(1, 0))
         send(f"a_dn{i + 1}", block, block, to_row(3, 0))
 
@@ -196,6 +200,9 @@
         dz = 4 - near[i - 1] if i else 0
         block = adjoints.at[row_of(3, dz)]
         arrived(f"a_up{i}", block)
+        if i in STRAIGHT:
+            arrived(f"a_dn{i}", adjoints.at[row_of(1, dz)])
+            return
         send(f"a_far_up{i}", block.at[upper], block.at[upper], to_row(1, 0))
         block = adjoints.at[row_of(1, dz)]
         arrived(f"a_dn{i}", block)
@@ -207,8 +214,8 @@
             arrived(f"s_y{dy}{h}", block)
             send(f"s_k{dy}{h}", block, block, to_col(0, 0, 1))
 
+    adjoint_onward(0)
     adjoint_far(0)
-    adjoint_onward(0)
     block = states.at[col_of(0, 1, 0)]
     arrived("s_z", block)
     for dy in (2, 1, 3):
@@ -218,11 +225,8 @@
     states_over(0)
     adjoint_onward(2)
     adjoint_far(1)
-    states_over(1)
     adjoint_far(2)
-    for h in (0, 1):
-        for dy in (0, 1, 3, 2):
-            arrived(f"s_k{dy}{h}", states.at[col_of(4 - dy, h, 1)])
+    adjoint_far(3)
 
     def forward(dx):
         first = ((x + dx) % 4) * 4
@@ -234,25 +238,41 @@
 
     zorder = [4 - near[2], 4 - near[1], 4 - near[0], 0]
 
-    def backward(dy):
-        first = ((y + dy) % 4) * 4
+    def backward(dys, h):
+        half_of = (zh + h) % 2
+        firsts = [((y + dy) % 4) * 4 + half_of * 2 for dy in dys]
         whole = jnp.concatenate([adjoints[i] for i in range(blocks)], axis=1)
-        start = pl.multiple_of(first * SIDE, SIDE)
+        lines = [dense[pl.ds(pl.multiple_of(first * SIDE, 2 * SIDE), 2 * SIDE), :] for first in firsts]
         product = lax.dot_general(
-            whole, dense[pl.ds(start, 4 * SIDE), :], (((1,), (1,)), ((), ())), preferred_element_type=F32
+            whole, jnp.concatenate(lines, axis=0), (((1,), (1,)), ((), ())), preferred_element_type=F32
         )
-        for i in range(4):
-            bpart[i % 2, first // 2 + i // 2] = product[:, i * SIDE : (i + 1) * SIDE].astype(BF16)
-        pair = pl.ds(((y + dy) % 4) * 2, 2)
-        send(f"b_k{dy}", bpart.at[1 - core, pair], bcore.at[pair], to_col(0, 0, 1))
-
-    def over_cores(dy):
-        first = ((y + dy) % 4) * 2
-        pair = pl.ds(first, 2)
-        arrived(f"b_k{dy}", bcore.at[pair])
-        for i in range(2):
-            bcore[first + i] = (bcore[first + i].astype(F32) + bpart[core, first + i].astype(F32)).astype(BF16)
-        send(f"b_y{dy}", bcore.at[pair], bring.at[dy - 1], to_col(dy, 0, 0))
+        for i, dy in enumerate(dys):
+            slot = firsts[i] // 2
+            for k in range(2):
+                part = product[:, (2 * i + k) * SIDE : (2 * i + k + 1) * SIDE]
+                bpart[k, slot] = part.astype(BF16)
+            send(f"b_k{dy}{h}", bpart.at[1 - core, slot], bcore.at[slot], to_col(0, 0, 1))
+
+    def over_cores(dy, h):
+        slot = ((y + dy) % 4) * 2 + (zh + h) % 2
+        arrived(f"b_k{dy}{h}", bcore.at[slot])
+        total = bcore[slot].astype(F32) + bpart[core, slot].astype(F32)
+        if dy:
+            bcore[slot] = total.astype(BF16)
+            send(f"b_y{dy}{h}", bcore.at[slot], bring.at[dy - 1, h], to_col(dy, 0, 0))
+        else:
+            btotal[h] = total
+
+    def ring_sum(h):
+        total = btotal[h]
+        for dy in (1, 3, 2):
+            arrived(f"b_y{dy}{h}", bring.at[dy - 1, h])
+            total += bring[dy - 1, h].astype(F32)
+        if h:
+            bsum[...] = total.astype(BF16)
+            send("b_z", bsum, bin_, to_col(0, 1, 0))
+        else:
+            btotal[0] = total
 
     def near_sum(i):
         dz = zorder[i]
@@ -265,31 +285,42 @@
         block[128:256] = (block[128:256].astype(F32) + fhalf_down[i].astype(F32)).astype(BF16)
         send(f"f_full_dn{i}", block, ffull_down.at[i], to_row(3, 0))
 
+    states_over(1)
+    for h in (0, 1):
+        for dy in (0, 1, 3, 2):
+            arrived(f"s_k{dy}{h}", states.at[col_of(4 - dy, h, 1)])
     forward(2)
     for i, dz in enumerate(zorder):
         block = fpart.at[row_of(2, dz)]
         send(f"f_half_up{i}", block.at[upper], fhalf_up.at[i], to_row(1, 0))
         send(f"f_half_dn{i}", block.at[lower], fhalf_down.at[i], to_row(3, 0))
-    adjoint_far(3)
+    for i in range(4):
+        block = adjoints.at[row_of(2, 4 - near[i - 1] if i else 0)]
+        if i in STRAIGHT:
+            arrived(f"a_x2{i}", block)
+        else:
+            arrived(f"a_far_up{i}", block.at[upper])
+            arrived(f"a_far_dn{i}", block.at[lower])
+    backward((2, 1), 1)
+    backward((3, 0), 1)
+    over_cores(2, 1)
+    over_cores(1, 1)
     forward(1)
     forward(3)
+    over_cores(3, 1)
+    over_cores(0, 1)
     near_sum(0)
     near_sum(1)
-
-    for i in range(4):
-        block = adjoints.at[row_of(2, 4 - near[i - 1] if i else 0)]
-        arrived(f"a_far_up{i}", block.at[upper])
-        arrived(f"a_far_dn{i}", block.at[lower])
-    backward(2)
+    backward((2, 1), 0)
     near_sum(2)
     near_sum(3)
-    backward(1)
-    over_cores(2)
-    backward(3)
-    over_cores(1)
+    backward((3, 0), 0)
+    over_cores(2, 0)
+    over_cores(1, 0)
+    over_cores(3, 0)
+    over_cores(0, 0)
+    ring_sum(1)
     forward(0)
-    over_cores(3)
-    backward(0)
 
     def forward_sum(i):
         arrived(f"f_full_up{i}", ffull_up.at[i])
@@ -302,24 +333,9 @@
         else:
             ftotal[...] = total
 
-    forward_sum(0)
-    forward_sum(1)
-    first = y * 2
-    arrived("b_k0", bcore.at[pl.ds(first, 2)])
-    for dy in (1, 3, 2):
-        arrived(f"b_y{dy}", bring.at[dy - 1])
-    for h in (1, 0):
-        n = (zh + h) % 2
-        total = bcore[first + n].astype(F32) + bpart[core, first + n].astype(F32)
-        for dy in (1, 2, 3):
-            total += bring[dy - 1, n].astype(F32)
-        if h:
-            bsum[...] = total.astype(BF16)
-            send("b_z", bsum, bin_, to_col(0, 1, 0))
-        else:
-            btotal[...] = total
-    forward_sum(2)
-    forward_sum(3)
+    for i in range(4):
+        forward_sum(i)
+    ring_sum(0)
 
     for copy in late_copies:
         copy.wait()
@@ -328,11 +344,13 @@
     for d in (1, 2, 3):
         arrived("f_z", fin.at[d - 1], d)
         total += fin[d - 1].astype(F32)
-    result[0] = fed + jnp.dot(mixing[...], total.astype(BF16), preferred_element_type=F32)
+    pre = fed + jnp.dot(mixing[...], total.astype(BF16), preferred_element_type=F32)
+    new_state[...] = jnp.tanh(pre).astype(BF16)
     arrived("b_z", bin_)
-    back = (btotal[...] + bin_[...].astype(F32)).astype(BF16)
+    back = (btotal[0] + bin_[...].astype(F32)).astype(BF16)
     pulled = lax.dot_general(mixing[...], back, (((0,), (0,)), ((), ())), preferred_element_type=F32)
-    result[1] = pulled + cotangent[...].astype(F32)
+    own = states[col].astype(F32)
+    new_adjoint[...] = ((1.0 - own * own) * (pulled + cotangent[...].astype(F32))).astype(BF16)
 
     for copy in sent:
         copy.wait_send()
@@ -345,14 +363,14 @@
     slots = slab.shape[0]
     hidden, nodes = state.shape
     vmem = pl.BlockSpec(memory_space=pltpu.VMEM)
-    anywhere = pl.BlockSpec(memory_space=pl.ANY)
+    anywhere = pl.BlockSpec(memory_space=pltpu.HBM)
     block = (hidden, nodes)
     half = (hidden // 2, nodes)
-    result = pl.pallas_call(
+    return pl.pallas_call(
         kernel,
-        out_shape=jax.ShapeDtypeStruct((2, *block), F32),
+        out_shape=(jax.ShapeDtypeStruct(block, BF16), jax.ShapeDtypeStruct(block, BF16)),
         in_specs=[anywhere] * 10,
-        out_specs=vmem,
+        out_specs=(vmem, vmem),
         scratch_shapes=[
             pltpu.VMEM((1, slots), jnp.int32),
             pltpu.VMEM((1, slots), jnp.int32),
@@ -378,7 +396,7 @@
             pltpu.VMEM((2, blocks // 2, *block), BF16),
             pltpu.VMEM((blocks // 2, *block), BF16),
             pltpu.VMEM((3, 2, *block), BF16),
-            pltpu.VMEM(block, F32),
+            pltpu.VMEM((2, *block), F32),
             pltpu.VMEM(block, BF16),
             pltpu.VMEM(block, BF16),
             pltpu.SemaphoreType.DMA((11,)),
@@ -386,26 +404,26 @@
             pltpu.SemaphoreType.DMA((COPIES,)),
         ],
         compiler_params=pltpu.CompilerParams(
-            collective_id=0, has_side_effects=True, vmem_limit_bytes=56 * 1024 * 1024
+            collective_id=0, has_side_effects=True, vmem_limit_bytes=26 * 1024 * 1024
         ),
         name="joint_step",
     )(
-        state,
-        adjoint,
-        slab,
-        tile_rows[0],
-        tile_cols[0],
-        live_tiles,
-        features,
-        cotangent,
-        mixing,
-        input_weight,
+        *(
+            a if a is live_tiles else pltpu.with_memory_space_constraint(a, pltpu.HBM)
+            for a in (
+                state,
+                adjoint,
+                slab,
+                tile_rows[0],
+                tile_cols[0],
+                live_tiles,
+                features,
+                cotangent,
+                mixing,
+                input_weight,
+            )
+        )
     )
-    new_state = jnp.tanh(result[0]).astype(BF16)
-    wide = state.astype(F32)
-    new_adjoint = ((1.0 - wide * wide) * result[1]).astype(BF16)
-    return new_state, new_adjoint
-
 
 def solution(mesh):
     placed = (

time: 54.1 us -> 48.5 us (0.90)
  Pallas kernels: 49.3 us -> 45.9 us
  other arithmetic: 3.11 us -> 0 us
  local copies, waits for them, and re-layouts: 0.01 us -> 1.26 us
    pallas_call x1, Pallas kernels: 49.3 us -> 45.9 us  [per_device(): pl.pallas_call(kernel, out_shape=(jax.ShapeDtypeStruct(block, BF16), jax....]
    convert_element_type x2 -> x0, other arithmetic: 3.11 us -> none  [the longest x1 1.56 us: per_device(): new_adjoint = ((1.0 - wide * wide) * result[1]).astype(BF16)]
    unnamed x2, local copies, waits for them, and re-layouts: 0.01 us -> 1.26 us
where the time goes in v4:
time: 48.5 us; the launch traced here: 48.4 us
  Pallas kernels  45.9 us (95%)
  between operations  1.29 us (3%)
  local copies, waits for them, and re-layouts  1.26 us (3%)
    pallas_call x1, Pallas kernels, per_device(): pl.pallas_call(kernel, out_shape=(jax.ShapeDtypeStruct(block, BF16), jax....  45.9 us
    unnamed x2, local copies, waits for them, and re-layouts  1.26 us

profile of v4, /device:TPU:32, one launch (start us, length us, event | category | flops | bytes accessed | tf_op | source)
XLA Modules:
  0.0 48.4 jit_solution(7594892441822755281)
XLA Ops:
  1.3 45.9 %joint_step.1 = (bf16[256,128]{1,0:T(8,128)(2,1)S(1)}, bf16[256,128]{1,0:T(8,128)(2,1)S(1)}) custom-call(bf16[256,128]{1,0:T(8,128)(2,1)} %state_hbm.1, bf16[256,128]{1,0:T(8,128)(2,1)} %adjoint_hbm.1, bf16[85,128,128]{2,1,0:T(8,128)(2,1)} %bitcast.3, s32[1,85]{1,0:T(1,128)} %bitcast.4, s32[1,85]{1,0:T(1,128)} %bitcast.5, s32[1,1]{1,0:T(1,128)S(6)} %copy.14.live_tiles_hbm, ...), custom_call_target="tpu_custom_call" | custom-call | tf_op jit(solution)/shard_map/joint_step/pallas_call | solution.py:369
  47.2 0.6 %copy.15 = bf16[256,128]{1,0:T(8,128)(2,1)} copy(bf16[256,128]{1,0:T(8,128)(2,1)S(1)} %get-tuple-element.4) | data formatting | bytes 131072
  47.8 0.6 %copy.16 = bf16[256,128]{1,0:T(8,128)(2,1)} copy(bf16[256,128]{1,0:T(8,128)(2,1)S(1)} %get-tuple-element.5) | data formatting | bytes 131072

commit v5 on v4

--- a/solution.py
+++ b/solution.py
@@ -168,10 +168,10 @@
     own_state, own_adjoint = states.at[col], adjoints.at[row]
     send("s_z", own_state, own_state, to_col(0, 1, 0))
     send("a_z", own_adjoint, own_adjoint, to_row(0, 4 - near[0]), 4 - near[0], 4)
+    send("a_z", own_adjoint, own_adjoint, to_row(0, 4 - near[1]), 4 - near[1], 4)
+    send("a_z", own_adjoint, own_adjoint, to_row(0, 4 - near[2]), 4 - near[2], 4)
     send("a_up0", own_adjoint, own_adjoint, to_row(1, 0))
     send("a_dn0", own_adjoint, own_adjoint, to_row(3, 0))
-    send("a_z", own_adjoint, own_adjoint, to_row(0, 4 - near[1]), 4 - near[1], 4)
-    send("a_z", own_adjoint, own_adjoint, to_row(0, 4 - near[2]), 4 - near[2], 4)
     for dy in (2, 1, 3):
         send(f"s_y{dy}0", own_state, own_state, to_col(dy, 0, 0))
     send("s_k00", own_state, own_state, to_col(0, 0, 1))
@@ -213,20 +213,6 @@
             block = states.at[col_of(4 - dy, h, 0)]
             arrived(f"s_y{dy}{h}", block)
             send(f"s_k{dy}{h}", block, block, to_col(0, 0, 1))
-
-    adjoint_onward(0)
-    adjoint_far(0)
-    block = states.at[col_of(0, 1, 0)]
-    arrived("s_z", block)
-    for dy in (2, 1, 3):
-        send(f"s_y{dy}1", block, block, to_col(dy, 0, 0))
-    send("s_k01", block, block, to_col(0, 0, 1))
-    adjoint_onward(1)
-    states_over(0)
-    adjoint_onward(2)
-    adjoint_far(1)
-    adjoint_far(2)
-    adjoint_far(3)
 
     def forward(dx):
         first = ((x + dx) % 4) * 4
@@ -285,6 +271,30 @@
         block[128:256] = (block[128:256].astype(F32) + fhalf_down[i].astype(F32)).astype(BF16)
         send(f"f_full_dn{i}", block, ffull_down.at[i], to_row(3, 0))
 
+    def forward_sum(i):
+        arrived(f"f_full_up{i}", ffull_up.at[i])
+        arrived(f"f_full_dn{i}", ffull_down.at[i])
+        dz = zorder[i]
+        total = fpart[row_of(0, dz)].astype(F32) + ffull_up[i].astype(F32) + ffull_down[i].astype(F32)
+        if i < 3:
+            fsum[i] = total.astype(BF16)
+            send("f_z", fsum.at[i], fin.at[dz - 1], to_row(0, dz), dz, 4)
+        else:
+            ftotal[...] = total
+
+    adjoint_onward(0)
+    adjoint_far(0)
+    block = states.at[col_of(0, 1, 0)]
+    arrived("s_z", block)
+    for dy in (2, 1, 3):
+        send(f"s_y{dy}1", block, block, to_col(dy, 0, 0))
+    send("s_k01", block, block, to_col(0, 0, 1))
+    adjoint_onward(1)
+    states_over(0)
+    adjoint_onward(2)
+    adjoint_far(1)
+    adjoint_far(2)
+    adjoint_far(3)
     states_over(1)
     for h in (0, 1):
         for dy in (0, 1, 3, 2):
@@ -321,20 +331,10 @@
     over_cores(0, 0)
     ring_sum(1)
     forward(0)
-
-    def forward_sum(i):
-        arrived(f"f_full_up{i}", ffull_up.at[i])
-        arrived(f"f_full_dn{i}", ffull_down.at[i])
-        dz = zorder[i]
-        total = fpart[row_of(0, dz)].astype(F32) + ffull_up[i].astype(F32) + ffull_down[i].astype(F32)
-        if i < 3:
-            fsum[i] = total.astype(BF16)
-            send("f_z", fsum.at[i], fin.at[dz - 1], to_row(0, dz), dz, 4)
-        else:
-            ftotal[...] = total
-
-    for i in range(4):
-        forward_sum(i)
+    forward_sum(0)
+    forward_sum(1)
+    forward_sum(2)
+    forward_sum(3)
     ring_sum(0)
 
     for copy in late_copies:

time: 48.5 us -> 48.5 us (level)
  no operation moved by 1% of the time
where the time goes in v5:
time: 48.5 us; the launch traced here: 48.4 us
  Pallas kernels  45.9 us (95%)
  between operations  1.29 us (3%)
  local copies, waits for them, and re-layouts  1.26 us (3%)
    pallas_call x1, Pallas kernels, per_device(): pl.pallas_call(kernel, out_shape=(jax.ShapeDtypeStruct(block, BF16), jax....  45.9 us
    unnamed x2, local copies, waits for them, and re-layouts  1.26 us

profile of v5, /device:TPU:32, one launch (start us, length us, event | category | flops | bytes accessed | tf_op | source)
XLA Modules:
  0.0 48.4 jit_solution(14137098821289246215)
XLA Ops:
  1.3 45.9 %joint_step.1 = (bf16[256,128]{1,0:T(8,128)(2,1)S(1)}, bf16[256,128]{1,0:T(8,128)(2,1)S(1)}) custom-call(bf16[256,128]{1,0:T(8,128)(2,1)} %state_hbm.1, bf16[256,128]{1,0:T(8,128)(2,1)} %adjoint_hbm.1, bf16[85,128,128]{2,1,0:T(8,128)(2,1)} %bitcast.3, s32[1,85]{1,0:T(1,128)} %bitcast.4, s32[1,85]{1,0:T(1,128)} %bitcast.5, s32[1,1]{1,0:T(1,128)S(6)} %copy.14.live_tiles_hbm, ...), custom_call_target="tpu_custom_call" | custom-call | tf_op jit(solution)/shard_map/joint_step/pallas_call | solution.py:369
  47.2 0.6 %copy.15 = bf16[256,128]{1,0:T(8,128)(2,1)} copy(bf16[256,128]{1,0:T(8,128)(2,1)S(1)} %get-tuple-element.4) | data formatting | bytes 131072
  47.8 0.6 %copy.16 = bf16[256,128]{1,0:T(8,128)(2,1)} copy(bf16[256,128]{1,0:T(8,128)(2,1)S(1)} %get-tuple-element.5) | data formatting | bytes 131072
